TPU v7x, 1024 devices: a whole 4x4x32 slice. The times are simulated.
1024 devices in a mesh: tm: 16 (over y, x_lo, core), space: 64 (over z, x_hi).
Axes of the slice: x: 4 (x_hi: 2, x_lo: 2; x = x_hi * 2 + x_lo), y: 4, z: 32, core: 2. Of those that a mesh axis runs over, the one named last changes fastest.
Arguments:
- dilution: int32 [8, 2], replicated, may hold values from 0 to 63, as said below
- eigvecs: float32 [2, 3, 16, 64, 13824], P(None, None, 'tm', None, 'space'), may hold values from -6 to 6
- gauge_links: float32 [16, 4, 2, 3, 3, 13824], P('tm', None, None, None, None, 'space'), may hold values from -2.4 to 2.4
- clover: float32 [16, 2, 2, 6, 6, 13824], P('tm', None, None, None, None, 'space'), may hold values from -0.14 to 1.34
Outputs:
- solutions: float32 [2, 4, 3, 16, 8, 13824], P(None, None, None, 'tm', None, 'space')
- perambulator: float32 [16, 64, 2, 4, 8], P('tm', 'space')
Inputs may be any that keep to these rules, and one draw needn't show every extreme that they name: `dilution`: column 0 of row s is the eigenvector of source s and column 1 its spin, 0 to 3; some row names eigenvector 64 - 1.
All inputs are finite; a program needn't handle non-finite values.
Results may differ from a plain program's by a relative error of at most 0.0003.
Values sent between devices are 32-bit elements; how exact they have to be, the bound alone decides.
No kernel may reach another device: no remote copies, remote signals or barrier semaphores. Data moves between devices by JAX's collectives and lax.ppermute only.
A program may use at most 128 MiB of HBM per device.

v0:
```python
import jax
import jax.numpy as jnp
from jax import lax
from jax.experimental import pallas as pl
from jax.experimental.pallas import tpu as pltpu
from jax.sharding import PartitionSpec as P

HOPPING = 0.125
RELAXATION = (0.9, 1.0, 1.1)
SITES = 216
LANES = 256
STRIDES = (36, 6, 1)
SPIN_BLOCKS = (
    ((0.0, -1j), (-1j, 0.0)),
    ((0.0, -1.0), (1.0, 0.0)),
    ((-1j, 0.0), (0.0, 1j)),
    ((1.0, 0.0), (0.0, 1.0)),
)
F32 = jnp.float32


def half(part, spin, colour):
    return (part * 2 + spin) * 3 + colour


def full(part, spin, colour):
    return (part * 4 + spin) * 3 + colour


def rotated(value, shift):
    shift %= LANES
    return value if shift == 0 else pltpu.roll(value, shift, axis=value.ndim - 1)


def add_turned(base, factor, real, imag):
    if factor == 1:
        return base[0] + real, base[1] + imag
    if factor == -1:
        return base[0] - real, base[1] - imag
    if factor == 1j:
        return base[0] - imag, base[1] + real
    return base[0] + imag, base[1] - real


def project(get, direction, parity):
    out = {}
    for spin in range(2):
        row = SPIN_BLOCKS[direction][spin]
        column = 0 if row[0] != 0 else 1
        factor = complex(parity * row[column])
        for colour in range(3):
            base = (get(0, spin, colour), get(1, spin, colour))
            real, imag = add_turned(base, factor, get(0, 2 + column, colour), get(1, 2 + column, colour))
            out[half(0, spin, colour)] = real
            out[half(1, spin, colour)] = imag
    return out


def turned(factor, real, imag):
    if factor == 1:
        return real, imag
    if factor == -1:
        return -real, -imag
    if factor == 1j:
        return -imag, real
    return imag, -real


def lower_of(direction, parity, spin):
    column = 0 if SPIN_BLOCKS[direction][0][spin] != 0 else 1
    return column, complex(parity * complex(SPIN_BLOCKS[direction][column][spin]).conjugate())


def rebuild(total, values, direction, parity):
    for spin in range(2):
        for colour in range(3):
            for part in range(2):
                q = full(part, spin, colour)
                total[q] = total[q] + values[half(part, spin, colour)]
    for spin in range(2):
        column, factor = lower_of(direction, parity, spin)
        for colour in range(3):
            q, r = full(0, 2 + spin, colour), full(1, 2 + spin, colour)
            total[q], total[r] = add_turned(
                (total[q], total[r]), factor, values[half(0, column, colour)], values[half(1, column, colour)]
            )


def rebuilt(values, direction, parity):
    out = {}
    for colour in range(3):
        for spin in range(2):
            for part in range(2):
                out[part, spin, colour] = values[half(part, spin, colour)]
            column, factor = lower_of(direction, parity, spin)
            out[0, 2 + spin, colour], out[1, 2 + spin, colour] = turned(
                factor, values[half(0, column, colour)], values[half(1, column, colour)]
            )
    return out


def link(links, direction, part, row, column):
    at = ((direction * 3 + row) * 3 + column) * 2 + part
    return jnp.broadcast_to(links[at : at + 1, :], (8, LANES))


def color_times(links, direction, values, adjoint):
    out = {}
    for row in range(3):
        for spin in range(2):
            real = imag = None
            for column in range(3):
                at = (column, row) if adjoint else (row, column)
                u_real = link(links, direction, 0, *at)
                u_imag = link(links, direction, 1, *at)
                v_real, v_imag = values[half(0, spin, column)], values[half(1, spin, column)]
                if adjoint:
                    a = u_real * v_real + u_imag * v_imag
                    b = u_real * v_imag - u_imag * v_real
                else:
                    a = u_real * v_real - u_imag * v_imag
                    b = u_real * v_imag + u_imag * v_real
                real = a if real is None else real + a
                imag = b if imag is None else imag + b
            out[half(0, spin, row)] = real
            out[half(1, spin, row)] = imag
    return out


def lane_slots():
    lane = lax.broadcasted_iota(jnp.int32, (8, LANES), 1)
    sixth = lane * 10923 >> 16
    x = sixth * 10923 >> 16
    return x, sixth - 6 * x, lane - 6 * sixth


def even_bits(dimension):
    bits = lax.axis_index("space") >> 2 * (2 - dimension)
    return ((bits ^ bits >> 1) & 1) == 0


def column_of(row):
    square = (8, 8)
    same = lax.broadcasted_iota(jnp.int32, square, 0) == lax.broadcasted_iota(jnp.int32, square, 1)
    return jnp.sum(jnp.where(same, jnp.broadcast_to(row.astype(F32), square), 0.0), axis=1, keepdims=True)


def place(sends, direction, vector, first, second):
    if direction == 0 and len(sends) == 5:
        number = lax.axis_index("space") >> 4
        sends[0][number ^ 1, vector] = first
        sends[0][number ^ 2, vector] = second
    else:
        sends[2 * direction - 6][vector] = first
        sends[2 * direction - 5][vector] = second


def arrived(received, direction, vector):
    if direction == 0 and len(received) == 5:
        number = lax.axis_index("space") >> 4
        first, second = received[0][number ^ 1, vector], received[0][number ^ 2, vector]
    else:
        first, second = received[2 * direction - 6][vector], received[2 * direction - 5][vector]
    low_is_ahead = even_bits(direction)
    return jnp.where(low_is_ahead, first, second), jnp.where(low_is_ahead, second, first)


def packed_low(values, slot, stride):
    out = values[0]
    for r in range(1, 6):
        out = jnp.where(slot == r, rotated(values[r], stride * r), out)
    return out


def packed_high(values, slot, stride):
    out = rotated(values[0], -5 * stride)
    for r in range(1, 6):
        out = jnp.where(slot == r, rotated(values[r], stride * (r - 5)), out)
    return out


def emit_faces(get, carried, sends):
    slots = lane_slots()
    for direction in range(3):
        stride, slot = STRIDES[direction], slots[direction]
        low_is_ahead = even_bits(direction)
        forward = project(get, direction, -1)
        for vector in range(2):
            own = range(6 * vector, 6 * vector + 6)
            low = packed_low([forward[q] for q in own], slot, stride)
            high = packed_high([carried[direction * 12 + q] for q in own], slot, stride)
            place(sends, direction, vector, jnp.where(low_is_ahead, high, low), jnp.where(low_is_ahead, low, high))


def emit_slices(get, links, slices):
    forward = project(get, 3, -1)
    backward = color_times(links, 3, project(get, 3, 1), True)
    for q in range(12):
        slices[0][q] = forward[q]
        slices[1][q] = backward[q]


def carry(get, links, carried):
    for direction in range(3):
        backward = color_times(links, direction, project(get, direction, 1), True)
        for q in range(12):
            carried[direction * 12 + q] = backward[q]


def pick_of(dilution):
    number = jnp.broadcast_to(column_of(dilution[0:1, :]), (8, 64)).astype(jnp.int32)
    return (lax.broadcasted_iota(jnp.int32, (8, 64), 1) == number).astype(F32)


def product(left, right, contracted):
    return lax.dot_general(
        left,
        right,
        ((contracted[:1], contracted[1:]), ((), ())),
        precision=lax.Precision.HIGHEST,
        preferred_element_type=F32,
    )


def masks_of(dilution):
    spins = jnp.broadcast_to(column_of(dilution[1:2, :]), (8, LANES))
    return [(spins == spin).astype(F32) for spin in range(4)]


def source_getter(chosen, masks):
    return lambda part, spin, colour: masks[spin] * chosen[part * 3 + colour]


def start_kernel(dilution, eigvecs, gauge, chosen, links, carried, *rest):
    sends, slices, later, basis = rest[:6], rest[6:8], rest[8], rest[9]
    held, copied = rest[10:13], rest[13]
    copies = [
        pltpu.make_async_copy(source, target, copied.at[n])
        for n, (source, target) in enumerate(zip((dilution, eigvecs, gauge), held))
    ]
    for copy in reversed(copies):
        copy.start()
    links[...] = jnp.zeros_like(links)
    basis[...] = jnp.zeros_like(basis)
    for copy in copies:
        copy.wait()
    dilution, eigvecs, gauge = held
    for direction in range(4):
        for row in range(3):
            for column in range(3):
                at = ((direction * 3 + row) * 3 + column) * 2
                links[at : at + 2, 0:SITES] = gauge[direction, row, column]
    pick = pick_of(dilution)
    for part in range(2):
        for colour in range(3):
            basis[part * 3 + colour, :, 0:SITES] = eigvecs[part, colour]
    for q in range(6):
        chosen[q] = product(pick, basis[q], (1, 0))
    slots = lane_slots()
    for direction in range(4):
        for group in range(-1, 8 if direction < 3 else 0):
            plain = [chosen[q] if group < 0 else basis[q, 8 * group : 8 * group + 8, :] for q in range(6)]
            times = []
            for part in range(2):
                for row in range(3):
                    total = None
                    for column in range(3):
                        u_real = link(links, direction, 0, column, row)
                        u_imag = link(links, direction, 1, column, row)
                        real, imag = plain[column], plain[3 + column]
                        term = u_real * real + u_imag * imag if part == 0 else u_real * imag - u_imag * real
                        total = term if total is None else total + term
                    times.append(total)
            if direction == 3:
                for q in range(6):
                    slices[0][q] = plain[q]
                    slices[1][q] = times[q]
                continue
            stride, slot = STRIDES[direction], slots[direction]
            low_is_ahead = even_bits(direction)
            low = packed_low(plain, slot, stride)
            high = packed_high(times, slot, stride)
            first, second = jnp.where(low_is_ahead, high, low), jnp.where(low_is_ahead, low, high)
            if group < 4:
                place(sends, direction, 1 + group, first, second)
            else:
                later[2 * direction, group - 4] = first
                later[2 * direction + 1, group - 4] = second
    carry(source_getter(chosen, masks_of(dilution)), links, carried)


def clover_kernel(clover, packed):
    packed[...] = jnp.zeros_like(packed)
    for part in range(2):
        for row in range(6):
            for column in range(6):
                at = ((part * 6 + row) * 6 + column) * 2
                packed[at : at + 2, 0:SITES] = clover[part, row, column]


def hop(total, links, get, carried, halos):
    total[...] = jnp.zeros_like(total)
    slots = lane_slots()
    for direction in range(3):
        stride, slot = STRIDES[direction], slots[direction]
        ahead, behind = halos[direction]
        if get is None and ahead is None:
            continue
        forward, backward = {}, {}
        if get is not None:
            for q, value in project(get, direction, -1).items():
                forward[q] = rotated(value, -stride)
                backward[q] = rotated(carried[direction * 12 + q], stride)
        for q in range(12):
            forward[q] = jnp.where(
                slot == 5, 0.0 if ahead is None else ahead[q], 0.0 if get is None else forward[q]
            )
            backward[q] = jnp.where(
                slot == 0, 0.0 if behind is None else behind[q], 0.0 if get is None else backward[q]
            )
        rebuild(total, color_times(links, direction, forward, False), direction, -1)
        rebuild(total, backward, direction, 1)
    ahead, behind = halos[3]
    if ahead is not None:
        rebuild(total, color_times(links, 3, ahead, False), 3, -1)
        rebuild(total, behind, 3, 1)


def slice_halos(slices):
    return [(None, None)] * 3 + [(slices[0], slices[1])]


def field_halos(received):
    halos = []
    for direction in range(3):
        stride = STRIDES[direction]
        ahead, behind = {}, {}
        for vector in range(2):
            from_ahead, from_behind = arrived(received, direction, vector)
            for r in range(6):
                ahead[6 * vector + r] = rotated(from_ahead, stride * (5 - r))
                behind[6 * vector + r] = rotated(from_behind, -stride * r)
        halos.append((ahead, behind))
    return halos


def basis_face(first, second, direction):
    both = [arrived(first, direction, 1 + group) for group in range(4)]
    both += [arrived(second, direction, 2 + group) for group in range(4)]
    return tuple(jnp.concatenate([pair[side] for pair in both], axis=0) for side in range(2))


def source_halos(received, slices, masks):
    halos = []
    for direction in range(4):
        if direction < 3:
            stride = STRIDES[direction]
            from_ahead, from_behind = arrived(received, direction, 0)
            ahead = [rotated(from_ahead, stride * (5 - r)) for r in range(6)]
            behind = [rotated(from_behind, -stride * r) for r in range(6)]
        else:
            ahead, behind = slices
        halos.append(
            (
                project(source_getter(ahead, masks), direction, -1),
                project(source_getter(behind, masks), direction, 1),
            )
        )
    return halos


def relax(weight, get, source, clover, total, store):
    for chiral in range(2):
        for row in range(6):
            real = imag = None
            for column in range(6):
                at = (row * 6 + column) * 2 + chiral
                a_real = jnp.broadcast_to(clover[at : at + 1, :], (8, LANES))
                a_imag = jnp.broadcast_to(clover[72 + at : 73 + at, :], (8, LANES))
                spin, colour = 2 * chiral + column // 3, column % 3
                v_real, v_imag = get(0, spin, colour), get(1, spin, colour)
                a = a_real * v_real - a_imag * v_imag
                b = a_real * v_imag + a_imag * v_real
                real = a if real is None else real + a
                imag = b if imag is None else imag + b
            spin, colour = 2 * chiral + row // 3, row % 3
            for part, applied in ((0, real), (1, imag)):
                q = full(part, spin, colour)
                store[q] = get(part, spin, colour) + weight * (
                    source(part, spin, colour) - (applied - HOPPING * total[q])
                )


def getter(ref):
    return lambda part, spin, colour: ref[full(part, spin, colour)]


def first_kernel(dilution, chosen, links, clover, carried_in, later, *rest):
    received, slices, psi, carried = rest[:6], rest[6:8], rest[8], rest[9]
    sends, next_slices, total = rest[10:16], rest[16:18], rest[18]
    masks = masks_of(dilution)
    source = source_getter(chosen, masks)
    hop(total, links, source, carried_in, source_halos(received, slices, masks))
    relax(RELAXATION[0], source, source, clover, total, psi)
    carry(getter(psi), links, carried)
    emit_faces(getter(psi), carried, sends)
    for direction in range(3):
        for group in range(4):
            place(sends, direction, 2 + group, later[2 * direction, group], later[2 * direction + 1, group])
    emit_slices(getter(psi), links, next_slices)


def projected_rows(values, place_at):
    rows = []
    for part in range(2):
        for spin in range(4):
            real = [values(part, spin, colour) for colour in range(3)]
            other = [values(1 - part, spin, colour) for colour in range(3)]
            if part == 1:
                other = [-value for value in other]
            rows.append(place_at(real, other))
    return rows


def projections(eigvecs, inner, psi, carried, first, second):
    summed = None
    rows = projected_rows(getter(inner), lambda real, other: real + other)
    for part in range(2):
        for colour in range(3):
            field = jnp.concatenate([row[3 * part + colour][:, 0:SITES] for row in rows], axis=0)
            term = product(eigvecs[part, colour], field, (1, 1))
            summed = term if summed is None else summed + term
    slots = lane_slots()
    inside = lax.broadcasted_iota(jnp.int32, (8, LANES), 1) < SITES
    faces = None
    for direction in range(3):
        stride, slot = STRIDES[direction], slots[direction]
        low = rebuilt(project(getter(psi), direction, -1), direction, -1)
        high = rebuilt([carried[direction * 12 + q] for q in range(12)], direction, 1)
        from_ahead, from_behind = basis_face(first, second, direction)
        for values, face, pack in ((low, from_behind, packed_low), (high, from_ahead, packed_high)):
            rows = projected_rows(
                lambda part, spin, colour: values[part, spin, colour],
                lambda real, other: jnp.where(inside, pack(real + other, slot, stride), 0.0),
            )
            term = product(face, jnp.concatenate(rows, axis=0), (1, 1))
            faces = term if faces is None else faces + term
    return summed + (RELAXATION[2] * HOPPING) * faces


def second_kernel(dilution, chosen, links, clover, spinor, carried_in, *rest):
    received, slices, (psi, carried, inner), next_slices, total = rest[:6], rest[6:8], rest[8:11], rest[11:13], rest[13]
    source = source_getter(chosen, masks_of(dilution))
    hop(total, links, getter(spinor), carried_in, field_halos(received) + [(slices[0], slices[1])])
    relax(RELAXATION[1], getter(spinor), source, clover, total, psi)
    emit_slices(getter(psi), links, next_slices)
    carry(getter(psi), links, carried)
    hop(total, links, getter(psi), carried, [(None, None)] * 4)
    relax(RELAXATION[2], getter(psi), source, clover, total, inner)


def project_kernel(links, eigvecs, psi, carried, inner_in, *rest):
    slices, first, second, inner, sends, total = rest[:2], rest[2:8], rest[8:14], rest[14], rest[15:20], rest[20]
    hop(total, links, None, None, slice_halos(slices))
    for q in range(24):
        inner[q] = inner_in[q] + (RELAXATION[2] * HOPPING) * total[q]
    sends[0][...] = jnp.zeros_like(sends[0])
    emit_faces(getter(psi), carried, sends)
    partial = projections(eigvecs, inner, psi, carried, first, second)
    for number in range(4):
        at = 16 * number
        sends[0][number, 2, :, 0:64] = partial[at : at + 8, :]
        sends[0][number, 2, :, 128:192] = partial[at + 8 : at + 16, :]


def line_sum_kernel(received, *rest):
    out = rest[-1]
    summed = received[0, 2]
    for number in range(1, 4):
        summed = summed + received[number, 2]
    out[0:8, :] = summed[:, 0:64]
    out[8:16, :] = summed[:, 128:192]


def last_kernel(links, inner, *rest):
    received, solutions, total = rest[:5], rest[5], rest[6]
    hop(total, links, None, None, field_halos(received) + [(None, None)])
    for q in range(24):
        solutions[q] = (inner[q] + (RELAXATION[2] * HOPPING) * total[q])[:, 0:SITES]


def call(kernel, outs, args, scratch=(), place=pltpu.VMEM):
    vmem = pl.BlockSpec(memory_space=pltpu.VMEM)
    return pl.pallas_call(
        kernel,
        out_shape=[jax.ShapeDtypeStruct(shape, F32) for shape in outs],
        in_specs=[pl.BlockSpec(memory_space=place)] * len(args),
        out_specs=[vmem] * len(outs),
        scratch_shapes=[pltpu.VMEM(shape, F32) if isinstance(shape, tuple) else shape for shape in scratch],
        compiler_params=pltpu.CompilerParams(vmem_limit_bytes=16 << 20),
    )(*args)


SLICES = [(12, 8, LANES)] * 2
FIELD = (24, 8, LANES)
CARRIED = (36, 8, LANES)


def faces_of(vectors):
    return [(vectors, 8, LANES)] * 6


BITS = (4, 5, 2, 3, 0, 1)


def flipped(value, n):
    return lax.ppermute(value, "space", [(i, i ^ 1 << BITS[n]) for i in range(lax.axis_size("space"))])


def on_line(value):
    lines = [[i + 16 * n for n in range(4)] for i in range(16)]
    return lax.all_to_all(value, "space", 0, 0, axis_index_groups=lines, tiled=True)


def shifted(slices):
    length = lax.axis_size("tm")
    out = []
    for n, by in enumerate((-1, 1)):
        out.append(lax.ppermute(slices[n], "tm", [(i, (i + by) % length) for i in range(length)]))
    return out


def exchanged(sends, slices):
    return [flipped(send, n) for n, send in enumerate(sends)], shifted(slices)


def body(dilution, eigvecs, gauge_links, clover):
    eigvecs = eigvecs[:, :, 0]
    dilution = dilution.T
    gauge_links = gauge_links.transpose(0, 1, 3, 4, 2, 5)
    clover = clover.transpose(0, 1, 3, 4, 2, 5)
    inputs = (dilution, eigvecs, gauge_links[0])
    chosen, links, carried, *sends, ahead, behind, later = call(
        start_kernel,
        [(6, 8, LANES), (72, LANES), CARRIED] + faces_of(5) + [(6, 8, LANES)] * 2 + [(6, 4, 8, LANES)],
        inputs,
        [(6, 64, LANES)]
        + [pltpu.VMEM(value.shape, value.dtype) for value in inputs]
        + [pltpu.SemaphoreType.DMA((3,))],
        pltpu.MemorySpace.HBM,
    )
    (packed,) = call(clover_kernel, [(144, LANES)], (clover[0],))
    first, slices = exchanged(sends, (ahead, behind))
    psi, carried, *sends, ahead, behind = call(
        first_kernel,
        [FIELD, CARRIED] + faces_of(6) + SLICES,
        (dilution, chosen, links, packed, carried, later, *first, *slices),
        [FIELD],
    )
    second, slices = exchanged(sends, (ahead, behind))
    psi, carried, inner, ahead, behind = call(
        second_kernel,
        [FIELD, CARRIED, FIELD] + SLICES,
        (dilution, chosen, links, packed, psi, carried, *second, *slices),
        [FIELD],
    )
    slices = shifted((ahead, behind))
    inner, *sends = call(
        project_kernel,
        [FIELD, (4, 3, 8, LANES)] + faces_of(2)[2:],
        (links, eigvecs, psi, carried, inner, *slices, *first, *second),
        [FIELD],
    )
    third = [on_line(sends[0])] + [flipped(send, n + 2) for n, send in enumerate(sends[1:])]
    (rows,) = call(line_sum_kernel, [(16, 64)], third)
    blocks = [[16 * n + i for i in range(16)] for n in range(4)]
    parts = lax.all_to_all(rows, "space", 0, 0, axis_index_groups=blocks, tiled=True)
    volume = SITES * lax.axis_size("space")
    reduced = jnp.sum(parts, axis=0) * (1.0 / (3.0 * volume))
    (solutions,) = call(last_kernel, [(24, 8, SITES)], (links, inner, *third), [FIELD])
    return solutions.reshape(2, 4, 3, 1, 8, SITES), reduced.reshape(1, 1, 2, 4, 8)


def solution(mesh):
    in_specs = (
        P(),
        P(None, None, "tm", None, "space"),
        P("tm", None, None, None, None, "space"),
        P("tm", None, None, None, None, "space"),
    )
    out_specs = (P(None, None, None, "tm", None, "space"), P("tm", "space", None, None, None))
    return jax.shard_map(body, mesh=mesh, in_specs=in_specs, out_specs=out_specs, check_vma=False)
```

profile of v0, /device:TPU:32, one launch (start us, length us, event | category | flops | bytes accessed | tf_op | source)
XLA Modules:
  0.0 179.6 jit_solution(4727728898412507897)
XLA Ops:
  0.6 0.0 copy-start.4
  0.6 0.7 copy-done.4
  1.3 0.0 copy-start
  1.3 1.0 copy-done
  2.3 0.0 copy-start.3
  2.3 0.9 copy-done.3
  3.2 1.4 shard_map.59
  4.6 15.7 %collective-permute-start = (f32[5,8,256]{2,1,0:T(8,128)S(1)}, f32[5,8,256]{2,1,0:T(8,128)S(1)}, u32[]{:S(2)}, u32[]{:S(2)}) collective-permute-start(f32[5,8,256]{2,1,0:T(8,128)S(1)} %get-tuple-element.39), channel_id=1, source_target_pairs={{0,16},{1,17},{2,18},{3,19},{4,20},{5,21},{6,22},{7,23},{8,24},{9,... | collective-permute-start | bytes 122888 | tf_op jit(solution)/shard_map/ppermute | solution.py:517
  20.3 18.5 %collective-permute-start.1 = (f32[5,8,256]{2,1,0:T(8,128)S(1)}, f32[5,8,256]{2,1,0:T(8,128)S(1)}, u32[]{:S(2)}, u32[]{:S(2)}) collective-permute-start(f32[5,8,256]{2,1,0:T(8,128)S(1)} %get-tuple-element.40), channel_id=1, source_target_pairs={{0,32},{1,33},{2,34},{3,35},{4,36},{5,37},{6,38},{7,39},{8,40},{9,... | collective-permute-start | bytes 122888 | tf_op jit(solution)/shard_map/ppermute | solution.py:517
  38.8 3.4 %collective-permute-start.2 = (f32[5,8,256]{2,1,0:T(8,128)S(1)}, f32[5,8,256]{2,1,0:T(8,128)S(1)}, u32[]{:S(2)}, u32[]{:S(2)}) collective-permute-start(f32[5,8,256]{2,1,0:T(8,128)S(1)} %get-tuple-element.41), channel_id=1, source_target_pairs={{0,4},{1,5},{2,6},{3,7},{4,0},{5,1},{6,2},{7,3},{8,12},{9,13},{10,... | collective-permute-start | bytes 122888 | tf_op jit(solution)/shard_map/ppermute | solution.py:517
  42.2 4.4 %collective-permute-start.6 = (f32[6,8,256]{2,1,0:T(8,128)S(1)}, f32[6,8,256]{2,1,0:T(8,128)S(1)}, u32[]{:S(2)}, u32[]{:S(2)}) collective-permute-start(f32[6,8,256]{2,1,0:T(8,128)S(1)} %get-tuple-element.45), channel_id=1, source_target_pairs={{0,960},{64,0},{128,64},{192,128},{256,192},{320,256},{384,320},{4... | collective-permute-start | bytes 147464 | tf_op jit(solution)/shard_map/ppermute | solution.py:529
  46.6 1.9 %collective-permute-start.7 = (f32[6,8,256]{2,1,0:T(8,128)S(1)}, f32[6,8,256]{2,1,0:T(8,128)S(1)}, u32[]{:S(2)}, u32[]{:S(2)}) collective-permute-start(f32[6,8,256]{2,1,0:T(8,128)S(1)} %get-tuple-element.46), channel_id=1, source_target_pairs={{0,64},{64,128},{128,192},{192,256},{256,320},{320,384},{384,448},... | collective-permute-start | bytes 147464 | tf_op jit(solution)/shard_map/ppermute | solution.py:529
  48.6 0.0 collective-permute-done.rest_0_.rest_2_
  48.6 4.3 %collective-permute-start.3 = (f32[5,8,256]{2,1,0:T(8,128)S(1)}, f32[5,8,256]{2,1,0:T(8,128)S(1)}, u32[]{:S(2)}, u32[]{:S(2)}) collective-permute-start(f32[5,8,256]{2,1,0:T(8,128)S(1)} %get-tuple-element.42), channel_id=1, source_target_pairs={{0,8},{1,9},{2,10},{3,11},{4,12},{5,13},{6,14},{7,15},{8,0},{9,1},... | collective-permute-start | bytes 122888 | tf_op jit(solution)/shard_map/ppermute | solution.py:517
  52.9 0.0 collective-permute-done.1.rest_1_.rest_3_
  52.9 4.6 %collective-permute-start.4 = (f32[5,8,256]{2,1,0:T(8,128)S(1)}, f32[5,8,256]{2,1,0:T(8,128)S(1)}, u32[]{:S(2)}, u32[]{:S(2)}) collective-permute-start(f32[5,8,256]{2,1,0:T(8,128)S(1)} %get-tuple-element.43), channel_id=1, source_target_pairs={{0,1},{1,0},{2,3},{3,2},{4,5},{5,4},{6,7},{7,6},{8,9},{9,8},{10,11... | collective-permute-start | bytes 122888 | tf_op jit(solution)/shard_map/ppermute | solution.py:517
  57.5 0.0 collective-permute-done.2.rest_2_.rest_4_
  57.5 2.9 %collective-permute-start.5 = (f32[5,8,256]{2,1,0:T(8,128)S(1)}, f32[5,8,256]{2,1,0:T(8,128)S(1)}, u32[]{:S(2)}, u32[]{:S(2)}) collective-permute-start(f32[5,8,256]{2,1,0:T(8,128)S(1)} %get-tuple-element.44), channel_id=1, source_target_pairs={{0,2},{1,3},{2,0},{3,1},{4,6},{5,7},{6,4},{7,5},{8,10},{9,11},{10,... | collective-permute-start | bytes 122888 | tf_op jit(solution)/shard_map/ppermute | solution.py:517
  60.5 0.0 copy-done.2
  60.5 0.1 shard_map.60.clover
  60.5 0.0 collective-permute-done.3.rest_3_.rest_5_
  60.6 0.0 collective-permute-done.4.rest_4_.rest_6_
  60.6 2.9 %collective-permute-done.5.rest_5_.rest_7_ = f32[5,8,256]{2,1,0:T(8,128)S(1)} collective-permute-done((f32[5,8,256]{2,1,0:T(8,128)S(1)}, f32[5,8,256]{2,1,0:T(8,128)S(1)}, u32[]{:S(2)}, u32[]{:S(2)}) %collective-permute-start.5) | collective-permute-done | bytes 40992 | tf_op jit(solution)/shard_map/ppermute | solution.py:517
  63.4 0.0 collective-permute-done.6.rest_6_
  63.4 0.0 collective-permute-done.7.rest_7_
  63.4 1.0 shard_map.61
  64.5 8.4 %collective-permute-start.8 = (f32[6,8,256]{2,1,0:T(8,128)S(1)}, f32[6,8,256]{2,1,0:T(8,128)S(1)}, u32[]{:S(2)}, u32[]{:S(2)}) collective-permute-start(f32[6,8,256]{2,1,0:T(8,128)S(1)} %get-tuple-element.49), channel_id=1, source_target_pairs={{0,16},{1,17},{2,18},{3,19},{4,20},{5,21},{6,22},{7,23},{8,24},{9,... | collective-permute-start | bytes 147464 | tf_op jit(solution)/shard_map/ppermute | solution.py:517
  72.9 13.6 %collective-permute-start.9 = (f32[6,8,256]{2,1,0:T(8,128)S(1)}, f32[6,8,256]{2,1,0:T(8,128)S(1)}, u32[]{:S(2)}, u32[]{:S(2)}) collective-permute-start(f32[6,8,256]{2,1,0:T(8,128)S(1)} %get-tuple-element.50), channel_id=1, source_target_pairs={{0,32},{1,33},{2,34},{3,35},{4,36},{5,37},{6,38},{7,39},{8,40},{9,... | collective-permute-start | bytes 147464 | tf_op jit(solution)/shard_map/ppermute | solution.py:517
  86.5 1.9 %collective-permute-start.10 = (f32[6,8,256]{2,1,0:T(8,128)S(1)}, f32[6,8,256]{2,1,0:T(8,128)S(1)}, u32[]{:S(2)}, u32[]{:S(2)}) collective-permute-start(f32[6,8,256]{2,1,0:T(8,128)S(1)} %get-tuple-element.51), channel_id=1, source_target_pairs={{0,4},{1,5},{2,6},{3,7},{4,0},{5,1},{6,2},{7,3},{8,12},{9,13},{10,... | collective-permute-start | bytes 147464 | tf_op jit(solution)/shard_map/ppermute | solution.py:517
  88.4 1.9 %collective-permute-start.14 = (f32[12,8,256]{2,1,0:T(8,128)S(1)}, f32[12,8,256]{2,1,0:T(8,128)S(1)}, u32[]{:S(2)}, u32[]{:S(2)}) collective-permute-start(f32[12,8,256]{2,1,0:T(8,128)S(1)} %get-tuple-element.55), channel_id=1, source_target_pairs={{0,960},{64,0},{128,64},{192,128},{256,192},{320,256},{384,320},{4... | collective-permute-start | bytes 294920 | tf_op jit(solution)/shard_map/ppermute | solution.py:529
  90.3 2.4 %collective-permute-start.15 = (f32[12,8,256]{2,1,0:T(8,128)S(1)}, f32[12,8,256]{2,1,0:T(8,128)S(1)}, u32[]{:S(2)}, u32[]{:S(2)}) collective-permute-start(f32[12,8,256]{2,1,0:T(8,128)S(1)} %get-tuple-element.56), channel_id=1, source_target_pairs={{0,64},{64,128},{128,192},{192,256},{256,320},{320,384},{384,448},... | collective-permute-start | bytes 294920 | tf_op jit(solution)/shard_map/ppermute | solution.py:529
  92.7 0.0 collective-permute-done.8.rest_0_.rest_8_
  92.8 4.7 %collective-permute-start.11 = (f32[6,8,256]{2,1,0:T(8,128)S(1)}, f32[6,8,256]{2,1,0:T(8,128)S(1)}, u32[]{:S(2)}, u32[]{:S(2)}) collective-permute-start(f32[6,8,256]{2,1,0:T(8,128)S(1)} %get-tuple-element.52), channel_id=1, source_target_pairs={{0,8},{1,9},{2,10},{3,11},{4,12},{5,13},{6,14},{7,15},{8,0},{9,1},... | collective-permute-start | bytes 147464 | tf_op jit(solution)/shard_map/ppermute | solution.py:517
  97.4 1.8 collective-permute-done.9.rest_1_.rest_9_
  99.2 2.7 %collective-permute-start.12 = (f32[6,8,256]{2,1,0:T(8,128)S(1)}, f32[6,8,256]{2,1,0:T(8,128)S(1)}, u32[]{:S(2)}, u32[]{:S(2)}) collective-permute-start(f32[6,8,256]{2,1,0:T(8,128)S(1)} %get-tuple-element.53), channel_id=1, source_target_pairs={{0,1},{1,0},{2,3},{3,2},{4,5},{5,4},{6,7},{7,6},{8,9},{9,8},{10,11... | collective-permute-start | bytes 147464 | tf_op jit(solution)/shard_map/ppermute | solution.py:517
  101.9 0.0 collective-permute-done.10.rest_2_.rest_10_
  101.9 6.5 %collective-permute-start.13 = (f32[6,8,256]{2,1,0:T(8,128)S(1)}, f32[6,8,256]{2,1,0:T(8,128)S(1)}, u32[]{:S(2)}, u32[]{:S(2)}) collective-permute-start(f32[6,8,256]{2,1,0:T(8,128)S(1)} %get-tuple-element.54), channel_id=1, source_target_pairs={{0,2},{1,3},{2,0},{3,1},{4,6},{5,7},{6,4},{7,5},{8,10},{9,11},{10,... | collective-permute-start | bytes 147464 | tf_op jit(solution)/shard_map/ppermute | solution.py:517
  108.4 0.0 collective-permute-done.11.rest_3_.rest_11_
  108.4 0.0 collective-permute-done.12.rest_4_.rest_12_
  108.4 2.0 %collective-permute-done.13.rest_5_.rest_13_ = f32[6,8,256]{2,1,0:T(8,128)S(1)} collective-permute-done((f32[6,8,256]{2,1,0:T(8,128)S(1)}, f32[6,8,256]{2,1,0:T(8,128)S(1)}, u32[]{:S(2)}, u32[]{:S(2)}) %collective-permute-start.13) | collective-permute-done | bytes 49184 | tf_op jit(solution)/shard_map/ppermute | solution.py:517
  110.4 0.0 collective-permute-done.14.rest_6_
  110.4 0.0 collective-permute-done.15.rest_7_
  110.4 1.4 shard_map.62
  111.9 1.9 %collective-permute-start.16 = (f32[12,8,256]{2,1,0:T(8,128)S(1)}, f32[12,8,256]{2,1,0:T(8,128)S(1)}, u32[]{:S(2)}, u32[]{:S(2)}) collective-permute-start(f32[12,8,256]{2,1,0:T(8,128)S(1)} %get-tuple-element.60), channel_id=1, source_target_pairs={{0,960},{64,0},{128,64},{192,128},{256,192},{320,256},{384,320},{4... | collective-permute-start | bytes 294920 | tf_op jit(solution)/shard_map/ppermute | solution.py:529
  113.8 2.4 %collective-permute-start.17 = (f32[12,8,256]{2,1,0:T(8,128)S(1)}, f32[12,8,256]{2,1,0:T(8,128)S(1)}, u32[]{:S(2)}, u32[]{:S(2)}) collective-permute-start(f32[12,8,256]{2,1,0:T(8,128)S(1)} %get-tuple-element.61), channel_id=1, source_target_pairs={{0,64},{64,128},{128,192},{192,256},{256,320},{320,384},{384,448},... | collective-permute-start | bytes 294920 | tf_op jit(solution)/shard_map/ppermute | solution.py:529
  116.2 0.0 collective-permute-done.16.rest_0_
  116.2 5.6 %collective-permute-done.17.rest_1_ = f32[12,8,256]{2,1,0:T(8,128)S(1)} collective-permute-done((f32[12,8,256]{2,1,0:T(8,128)S(1)}, f32[12,8,256]{2,1,0:T(8,128)S(1)}, u32[]{:S(2)}, u32[]{:S(2)}) %collective-permute-start.17) | collective-permute-done | bytes 98336 | tf_op jit(solution)/shard_map/ppermute | solution.py:529
  121.9 0.0 copy-done.1
  121.9 1.7 shard_map.63
  123.6 12.9 %all-to-all-start = ((f32[4,3,8,256]{3,2,1,0:T(8,128)}), f32[4,3,8,256]{3,2,1,0:T(8,128)S(1)}, u32[]{:S(2)}, u32[]{:S(2)}) async-start(f32[4,3,8,256]{3,2,1,0:T(8,128)} %get-tuple-element.63), calls=%async_computation | async-start | bytes 196608 | tf_op jit(solution)/shard_map/all_to_all | solution.py:522
  136.5 1.9 %collective-permute-start.18 = (f32[2,8,256]{2,1,0:T(8,128)S(1)}, f32[2,8,256]{2,1,0:T(8,128)S(1)}, u32[]{:S(2)}, u32[]{:S(2)}) collective-permute-start(f32[2,8,256]{2,1,0:T(8,128)S(1)} %get-tuple-element.64), channel_id=1, source_target_pairs={{0,4},{1,5},{2,6},{3,7},{4,0},{5,1},{6,2},{7,3},{8,12},{9,13},{10,... | collective-permute-start | bytes 49160 | tf_op jit(solution)/shard_map/ppermute | solution.py:517
  138.4 3.7 %collective-permute-start.19 = (f32[2,8,256]{2,1,0:T(8,128)S(1)}, f32[2,8,256]{2,1,0:T(8,128)S(1)}, u32[]{:S(2)}, u32[]{:S(2)}) collective-permute-start(f32[2,8,256]{2,1,0:T(8,128)S(1)} %get-tuple-element.65), channel_id=1, source_target_pairs={{0,8},{1,9},{2,10},{3,11},{4,12},{5,13},{6,14},{7,15},{8,0},{9,1},... | collective-permute-start | bytes 49160 | tf_op jit(solution)/shard_map/ppermute | solution.py:517
  142.1 4.6 %collective-permute-start.20 = (f32[2,8,256]{2,1,0:T(8,128)S(1)}, f32[2,8,256]{2,1,0:T(8,128)S(1)}, u32[]{:S(2)}, u32[]{:S(2)}) collective-permute-start(f32[2,8,256]{2,1,0:T(8,128)S(1)} %get-tuple-element.66), channel_id=1, source_target_pairs={{0,1},{1,0},{2,3},{3,2},{4,5},{5,4},{6,7},{7,6},{8,9},{9,8},{10,11... | collective-permute-start | bytes 49160 | tf_op jit(solution)/shard_map/ppermute | solution.py:517
  146.8 3.5 %collective-permute-start.21 = (f32[2,8,256]{2,1,0:T(8,128)S(1)}, f32[2,8,256]{2,1,0:T(8,128)S(1)}, u32[]{:S(2)}, u32[]{:S(2)}) collective-permute-start(f32[2,8,256]{2,1,0:T(8,128)S(1)} %get-tuple-element.67), channel_id=1, source_target_pairs={{0,2},{1,3},{2,0},{3,1},{4,6},{5,7},{6,4},{7,5},{8,10},{9,11},{10,... | collective-permute-start | bytes 49160 | tf_op jit(solution)/shard_map/ppermute | solution.py:517
  150.3 0.0 collective-permute-done.18.rest_1_.rest_0_
  150.3 0.0 collective-permute-done.19.rest_2_.rest_1_
  150.3 0.0 collective-permute-done.20.rest_3_.rest_2_
  150.3 2.1 %collective-permute-done.21.rest_4_.rest_3_ = f32[2,8,256]{2,1,0:T(8,128)S(1)} collective-permute-done((f32[2,8,256]{2,1,0:T(8,128)S(1)}, f32[2,8,256]{2,1,0:T(8,128)S(1)}, u32[]{:S(2)}, u32[]{:S(2)}) %collective-permute-start.21) | collective-permute-done | bytes 16416 | tf_op jit(solution)/shard_map/ppermute | solution.py:517
  152.4 8.8 %all-to-all-done.rest_0_.received = f32[4,3,8,256]{3,2,1,0:T(8,128)S(1)} async-done(((f32[4,3,8,256]{3,2,1,0:T(8,128)}), f32[4,3,8,256]{3,2,1,0:T(8,128)S(1)}, u32[]{:S(2)}, u32[]{:S(2)}) %all-to-all-start) | async-done | bytes 98336 | tf_op jit(solution)/shard_map/all_to_all | solution.py:522
  161.1 0.6 shard_map.65
  161.7 5.7 %all-to-all-start.1 = ((f32[16,1,64]{2,1,0:T(1,128)}), f32[16,1,64]{2,1,0:T(1,128)S(1)}, u32[]{:S(2)}, u32[]{:S(2)}) async-start(f32[16,1,64]{2,1,0:T(1,128)} %bitcast.9), calls=%async_computation.1 | async-start | bytes 16384 | tf_op jit(solution)/shard_map/all_to_all | solution.py:577
  167.5 1.0 shard_map.64
  168.5 10.4 %all-to-all-done.1 = f32[16,1,64]{2,1,0:T(1,128)S(1)} async-done(((f32[16,1,64]{2,1,0:T(1,128)}), f32[16,1,64]{2,1,0:T(1,128)S(1)}, u32[]{:S(2)}, u32[]{:S(2)}) %all-to-all-start.1) | async-done | bytes 4128 | tf_op jit(solution)/shard_map/all_to_all | solution.py:577
  178.9 0.7 mul.18
  (4 shorter events, 0.0 us)
Async XLA Ops:
  0.6 0.7 copy-start.4
  1.3 1.0 copy-start
  2.3 0.9 copy-start.3
  3.2 57.3 %copy-start.2 = (f32[1,2,2,6,6,216]{5,2,4,3,1,0:T(2,128)S(1)}, f32[1,2,2,6,6,216]{5,2,4,3,1,0:T(2,128)}, u32[]{:S(2)}) copy-start(f32[1,2,2,6,6,216]{5,2,4,3,1,0:T(2,128)} %param.7) | copy-start | bytes 373252
  4.6 44.0 %collective-permute-start = (f32[5,8,256]{2,1,0:T(8,128)S(1)}, f32[5,8,256]{2,1,0:T(8,128)S(1)}, u32[]{:S(2)}, u32[]{:S(2)}) collective-permute-start(f32[5,8,256]{2,1,0:T(8,128)S(1)} %get-tuple-element.39), channel_id=1, source_target_pairs={{0,16},{1,17},{2,18},{3,19},{4,20},{5,21},{6,22},{7,23},{8,24},{9,... | collective-permute-start | bytes 122888 | tf_op jit(solution)/shard_map/ppermute | solution.py:517
  20.3 32.6 %collective-permute-start.1 = (f32[5,8,256]{2,1,0:T(8,128)S(1)}, f32[5,8,256]{2,1,0:T(8,128)S(1)}, u32[]{:S(2)}, u32[]{:S(2)}) collective-permute-start(f32[5,8,256]{2,1,0:T(8,128)S(1)} %get-tuple-element.40), channel_id=1, source_target_pairs={{0,32},{1,33},{2,34},{3,35},{4,36},{5,37},{6,38},{7,39},{8,40},{9,... | collective-permute-start | bytes 122888 | tf_op jit(solution)/shard_map/ppermute | solution.py:517
  38.8 18.7 %collective-permute-start.2 = (f32[5,8,256]{2,1,0:T(8,128)S(1)}, f32[5,8,256]{2,1,0:T(8,128)S(1)}, u32[]{:S(2)}, u32[]{:S(2)}) collective-permute-start(f32[5,8,256]{2,1,0:T(8,128)S(1)} %get-tuple-element.41), channel_id=1, source_target_pairs={{0,4},{1,5},{2,6},{3,7},{4,0},{5,1},{6,2},{7,3},{8,12},{9,13},{10,... | collective-permute-start | bytes 122888 | tf_op jit(solution)/shard_map/ppermute | solution.py:517
  42.2 21.3 %collective-permute-start.6 = (f32[6,8,256]{2,1,0:T(8,128)S(1)}, f32[6,8,256]{2,1,0:T(8,128)S(1)}, u32[]{:S(2)}, u32[]{:S(2)}) collective-permute-start(f32[6,8,256]{2,1,0:T(8,128)S(1)} %get-tuple-element.45), channel_id=1, source_target_pairs={{0,960},{64,0},{128,64},{192,128},{256,192},{320,256},{384,320},{4... | collective-permute-start | bytes 147464 | tf_op jit(solution)/shard_map/ppermute | solution.py:529
  46.6 16.8 %collective-permute-start.7 = (f32[6,8,256]{2,1,0:T(8,128)S(1)}, f32[6,8,256]{2,1,0:T(8,128)S(1)}, u32[]{:S(2)}, u32[]{:S(2)}) collective-permute-start(f32[6,8,256]{2,1,0:T(8,128)S(1)} %get-tuple-element.46), channel_id=1, source_target_pairs={{0,64},{64,128},{128,192},{192,256},{256,320},{320,384},{384,448},... | collective-permute-start | bytes 147464 | tf_op jit(solution)/shard_map/ppermute | solution.py:529
  48.6 12.0 %collective-permute-start.3 = (f32[5,8,256]{2,1,0:T(8,128)S(1)}, f32[5,8,256]{2,1,0:T(8,128)S(1)}, u32[]{:S(2)}, u32[]{:S(2)}) collective-permute-start(f32[5,8,256]{2,1,0:T(8,128)S(1)} %get-tuple-element.42), channel_id=1, source_target_pairs={{0,8},{1,9},{2,10},{3,11},{4,12},{5,13},{6,14},{7,15},{8,0},{9,1},... | collective-permute-start | bytes 122888 | tf_op jit(solution)/shard_map/ppermute | solution.py:517
  52.9 7.7 %collective-permute-start.4 = (f32[5,8,256]{2,1,0:T(8,128)S(1)}, f32[5,8,256]{2,1,0:T(8,128)S(1)}, u32[]{:S(2)}, u32[]{:S(2)}) collective-permute-start(f32[5,8,256]{2,1,0:T(8,128)S(1)} %get-tuple-element.43), channel_id=1, source_target_pairs={{0,1},{1,0},{2,3},{3,2},{4,5},{5,4},{6,7},{7,6},{8,9},{9,8},{10,11... | collective-permute-start | bytes 122888 | tf_op jit(solution)/shard_map/ppermute | solution.py:517
  57.5 5.9 %collective-permute-start.5 = (f32[5,8,256]{2,1,0:T(8,128)S(1)}, f32[5,8,256]{2,1,0:T(8,128)S(1)}, u32[]{:S(2)}, u32[]{:S(2)}) collective-permute-start(f32[5,8,256]{2,1,0:T(8,128)S(1)} %get-tuple-element.44), channel_id=1, source_target_pairs={{0,2},{1,3},{2,0},{3,1},{4,6},{5,7},{6,4},{7,5},{8,10},{9,11},{10,... | collective-permute-start | bytes 122888 | tf_op jit(solution)/shard_map/ppermute | solution.py:517
  64.5 28.3 %collective-permute-start.8 = (f32[6,8,256]{2,1,0:T(8,128)S(1)}, f32[6,8,256]{2,1,0:T(8,128)S(1)}, u32[]{:S(2)}, u32[]{:S(2)}) collective-permute-start(f32[6,8,256]{2,1,0:T(8,128)S(1)} %get-tuple-element.49), channel_id=1, source_target_pairs={{0,16},{1,17},{2,18},{3,19},{4,20},{5,21},{6,22},{7,23},{8,24},{9,... | collective-permute-start | bytes 147464 | tf_op jit(solution)/shard_map/ppermute | solution.py:517
  72.9 26.3 %collective-permute-start.9 = (f32[6,8,256]{2,1,0:T(8,128)S(1)}, f32[6,8,256]{2,1,0:T(8,128)S(1)}, u32[]{:S(2)}, u32[]{:S(2)}) collective-permute-start(f32[6,8,256]{2,1,0:T(8,128)S(1)} %get-tuple-element.50), channel_id=1, source_target_pairs={{0,32},{1,33},{2,34},{3,35},{4,36},{5,37},{6,38},{7,39},{8,40},{9,... | collective-permute-start | bytes 147464 | tf_op jit(solution)/shard_map/ppermute | solution.py:517
  86.5 15.4 %collective-permute-start.10 = (f32[6,8,256]{2,1,0:T(8,128)S(1)}, f32[6,8,256]{2,1,0:T(8,128)S(1)}, u32[]{:S(2)}, u32[]{:S(2)}) collective-permute-start(f32[6,8,256]{2,1,0:T(8,128)S(1)} %get-tuple-element.51), channel_id=1, source_target_pairs={{0,4},{1,5},{2,6},{3,7},{4,0},{5,1},{6,2},{7,3},{8,12},{9,13},{10,... | collective-permute-start | bytes 147464 | tf_op jit(solution)/shard_map/ppermute | solution.py:517
  88.4 22.0 %collective-permute-start.14 = (f32[12,8,256]{2,1,0:T(8,128)S(1)}, f32[12,8,256]{2,1,0:T(8,128)S(1)}, u32[]{:S(2)}, u32[]{:S(2)}) collective-permute-start(f32[12,8,256]{2,1,0:T(8,128)S(1)} %get-tuple-element.55), channel_id=1, source_target_pairs={{0,960},{64,0},{128,64},{192,128},{256,192},{320,256},{384,320},{4... | collective-permute-start | bytes 294920 | tf_op jit(solution)/shard_map/ppermute | solution.py:529
  90.3 20.1 %collective-permute-start.15 = (f32[12,8,256]{2,1,0:T(8,128)S(1)}, f32[12,8,256]{2,1,0:T(8,128)S(1)}, u32[]{:S(2)}, u32[]{:S(2)}) collective-permute-start(f32[12,8,256]{2,1,0:T(8,128)S(1)} %get-tuple-element.56), channel_id=1, source_target_pairs={{0,64},{64,128},{128,192},{192,256},{256,320},{320,384},{384,448},... | collective-permute-start | bytes 294920 | tf_op jit(solution)/shard_map/ppermute | solution.py:529
  92.8 15.6 %collective-permute-start.11 = (f32[6,8,256]{2,1,0:T(8,128)S(1)}, f32[6,8,256]{2,1,0:T(8,128)S(1)}, u32[]{:S(2)}, u32[]{:S(2)}) collective-permute-start(f32[6,8,256]{2,1,0:T(8,128)S(1)} %get-tuple-element.52), channel_id=1, source_target_pairs={{0,8},{1,9},{2,10},{3,11},{4,12},{5,13},{6,14},{7,15},{8,0},{9,1},... | collective-permute-start | bytes 147464 | tf_op jit(solution)/shard_map/ppermute | solution.py:517
  99.2 9.2 %collective-permute-start.12 = (f32[6,8,256]{2,1,0:T(8,128)S(1)}, f32[6,8,256]{2,1,0:T(8,128)S(1)}, u32[]{:S(2)}, u32[]{:S(2)}) collective-permute-start(f32[6,8,256]{2,1,0:T(8,128)S(1)} %get-tuple-element.53), channel_id=1, source_target_pairs={{0,1},{1,0},{2,3},{3,2},{4,5},{5,4},{6,7},{7,6},{8,9},{9,8},{10,11... | collective-permute-start | bytes 147464 | tf_op jit(solution)/shard_map/ppermute | solution.py:517
  101.9 8.5 %collective-permute-start.13 = (f32[6,8,256]{2,1,0:T(8,128)S(1)}, f32[6,8,256]{2,1,0:T(8,128)S(1)}, u32[]{:S(2)}, u32[]{:S(2)}) collective-permute-start(f32[6,8,256]{2,1,0:T(8,128)S(1)} %get-tuple-element.54), channel_id=1, source_target_pairs={{0,2},{1,3},{2,0},{3,1},{4,6},{5,7},{6,4},{7,5},{8,10},{9,11},{10,... | collective-permute-start | bytes 147464 | tf_op jit(solution)/shard_map/ppermute | solution.py:517
  110.4 11.4 %copy-start.1 = (f32[2,3,1,64,216]{4,3,2,1,0:T(8,128)S(1)}, f32[2,3,1,64,216]{4,3,2,1,0:T(8,128)}, u32[]{:S(2)}) copy-start(f32[2,3,1,64,216]{4,3,2,1,0:T(8,128)} %param.5) | copy-start | bytes 995332
  111.9 4.3 %collective-permute-start.16 = (f32[12,8,256]{2,1,0:T(8,128)S(1)}, f32[12,8,256]{2,1,0:T(8,128)S(1)}, u32[]{:S(2)}, u32[]{:S(2)}) collective-permute-start(f32[12,8,256]{2,1,0:T(8,128)S(1)} %get-tuple-element.60), channel_id=1, source_target_pairs={{0,960},{64,0},{128,64},{192,128},{256,192},{320,256},{384,320},{4... | collective-permute-start | bytes 294920 | tf_op jit(solution)/shard_map/ppermute | solution.py:529
  113.8 8.0 %collective-permute-start.17 = (f32[12,8,256]{2,1,0:T(8,128)S(1)}, f32[12,8,256]{2,1,0:T(8,128)S(1)}, u32[]{:S(2)}, u32[]{:S(2)}) collective-permute-start(f32[12,8,256]{2,1,0:T(8,128)S(1)} %get-tuple-element.61), channel_id=1, source_target_pairs={{0,64},{64,128},{128,192},{192,256},{256,320},{320,384},{384,448},... | collective-permute-start | bytes 294920 | tf_op jit(solution)/shard_map/ppermute | solution.py:529
  123.6 37.6 %all-to-all-start = ((f32[4,3,8,256]{3,2,1,0:T(8,128)}), f32[4,3,8,256]{3,2,1,0:T(8,128)S(1)}, u32[]{:S(2)}, u32[]{:S(2)}) async-start(f32[4,3,8,256]{3,2,1,0:T(8,128)} %get-tuple-element.63), calls=%async_computation | async-start | bytes 196608 | tf_op jit(solution)/shard_map/all_to_all | solution.py:522
  136.5 13.8 %collective-permute-start.18 = (f32[2,8,256]{2,1,0:T(8,128)S(1)}, f32[2,8,256]{2,1,0:T(8,128)S(1)}, u32[]{:S(2)}, u32[]{:S(2)}) collective-permute-start(f32[2,8,256]{2,1,0:T(8,128)S(1)} %get-tuple-element.64), channel_id=1, source_target_pairs={{0,4},{1,5},{2,6},{3,7},{4,0},{5,1},{6,2},{7,3},{8,12},{9,13},{10,... | collective-permute-start | bytes 49160 | tf_op jit(solution)/shard_map/ppermute | solution.py:517
  138.4 11.9 %collective-permute-start.19 = (f32[2,8,256]{2,1,0:T(8,128)S(1)}, f32[2,8,256]{2,1,0:T(8,128)S(1)}, u32[]{:S(2)}, u32[]{:S(2)}) collective-permute-start(f32[2,8,256]{2,1,0:T(8,128)S(1)} %get-tuple-element.65), channel_id=1, source_target_pairs={{0,8},{1,9},{2,10},{3,11},{4,12},{5,13},{6,14},{7,15},{8,0},{9,1},... | collective-permute-start | bytes 49160 | tf_op jit(solution)/shard_map/ppermute | solution.py:517
  142.1 8.2 %collective-permute-start.20 = (f32[2,8,256]{2,1,0:T(8,128)S(1)}, f32[2,8,256]{2,1,0:T(8,128)S(1)}, u32[]{:S(2)}, u32[]{:S(2)}) collective-permute-start(f32[2,8,256]{2,1,0:T(8,128)S(1)} %get-tuple-element.66), channel_id=1, source_target_pairs={{0,1},{1,0},{2,3},{3,2},{4,5},{5,4},{6,7},{7,6},{8,9},{9,8},{10,11... | collective-permute-start | bytes 49160 | tf_op jit(solution)/shard_map/ppermute | solution.py:517
  146.8 5.6 %collective-permute-start.21 = (f32[2,8,256]{2,1,0:T(8,128)S(1)}, f32[2,8,256]{2,1,0:T(8,128)S(1)}, u32[]{:S(2)}, u32[]{:S(2)}) collective-permute-start(f32[2,8,256]{2,1,0:T(8,128)S(1)} %get-tuple-element.67), channel_id=1, source_target_pairs={{0,2},{1,3},{2,0},{3,1},{4,6},{5,7},{6,4},{7,5},{8,10},{9,11},{10,... | collective-permute-start | bytes 49160 | tf_op jit(solution)/shard_map/ppermute | solution.py:517
  161.7 17.1 %all-to-all-start.1 = ((f32[16,1,64]{2,1,0:T(1,128)}), f32[16,1,64]{2,1,0:T(1,128)S(1)}, u32[]{:S(2)}, u32[]{:S(2)}) async-start(f32[16,1,64]{2,1,0:T(1,128)} %bitcast.9), calls=%async_computation.1 | async-start | bytes 16384 | tf_op jit(solution)/shard_map/all_to_all | solution.py:577
where the time goes:
time: 181 us; the launch traced here: 180 us
  starting transfers between devices  135 us (75%)
  waiting for transfers between devices  33.5 us (19%)
  Pallas kernels  7.19 us (4%)
  local copies, waits for them, and re-layouts  3.24 us (2%)
    ppermute x16, starting transfers between devices, flipped(): lax.ppermute(value, 'space', [(i, i ^ 1 << BITS[n]) for i in range(lax.ax...  101 us
    ppermute x6, starting transfers between devices, shifted(): lax.ppermute(slices[n], 'tm', [(i, (i + by) % length) for i in range(leng...  15 us
    all_to_all x1, starting transfers between devices, on_line(): lax.all_to_all(value, 'space', 0, 0, axis_index_groups=lines, tiled=True)  12.9 us
    all_to_all x1, waiting for transfers between devices, body(): lax.all_to_all(rows, 'space', 0, 0, axis_index_groups=blocks, tiled=True)  10.4 us
    ppermute x16, waiting for transfers between devices, flipped(): lax.ppermute(value, 'space', [(i, i ^ 1 << BITS[n]) for i in range(lax.ax...  8.77 us
    all_to_all x1, waiting for transfers between devices, on_line(): lax.all_to_all(value, 'space', 0, 0, axis_index_groups=lines, tiled=True)  8.76 us
    pallas_call x7, Pallas kernels, call(): pl.pallas_call(kernel, out_shape=[jax.ShapeDtypeStruct(shape, F32) for sh...  7.19 us
    all_to_all x1, starting transfers between devices, body(): lax.all_to_all(rows, 'space', 0, 0, axis_index_groups=blocks, tiled=True)  5.74 us
  transfers between devices with their start and end apart: 24, of which 7 were waited for; matrix products, arithmetic and copies ran while one was open for 0% of the time, Pallas kernels for 1%

commit v1 on v0

--- a/solution.py
+++ b/solution.py
@@ -1,3 +1,5 @@
+import functools
+
 import jax
 import jax.numpy as jnp
 from jax import lax
@@ -449,44 +451,57 @@
 
 
 def second_kernel(dilution, chosen, links, clover, spinor, carried_in, *rest):
-    received, slices, (psi, carried, inner), next_slices, total = rest[:6], rest[6:8], rest[8:11], rest[11:13], rest[13]
+    received, slices, (psi, carried, inner), next_slices = rest[:6], rest[6:8], rest[8:11], rest[11:13]
+    (x_faces, *sends), total = rest[13:18], rest[18]
     source = source_getter(chosen, masks_of(dilution))
     hop(total, links, getter(spinor), carried_in, field_halos(received) + [(slices[0], slices[1])])
     relax(RELAXATION[1], getter(spinor), source, clover, total, psi)
     emit_slices(getter(psi), links, next_slices)
     carry(getter(psi), links, carried)
+    emit_faces(getter(psi), carried, [x_faces.at[0], x_faces.at[1], *sends])
     hop(total, links, getter(psi), carried, [(None, None)] * 4)
     relax(RELAXATION[2], getter(psi), source, clover, total, inner)
 
 
 def project_kernel(links, eigvecs, psi, carried, inner_in, *rest):
-    slices, first, second, inner, sends, total = rest[:2], rest[2:8], rest[8:14], rest[14], rest[15:20], rest[20]
+    slices, first, second, faces = rest[:2], rest[2:8], rest[8:14], rest[14:17]
+    inner, partial, faces_out, total = rest[17], rest[18], rest[19:22], rest[22]
     hop(total, links, None, None, slice_halos(slices))
     for q in range(24):
         inner[q] = inner_in[q] + (RELAXATION[2] * HOPPING) * total[q]
-    sends[0][...] = jnp.zeros_like(sends[0])
-    emit_faces(getter(psi), carried, sends)
-    partial = projections(eigvecs, inner, psi, carried, first, second)
-    for number in range(4):
-        at = 16 * number
-        sends[0][number, 2, :, 0:64] = partial[at : at + 8, :]
-        sends[0][number, 2, :, 128:192] = partial[at + 8 : at + 16, :]
-
-
-def line_sum_kernel(received, *rest):
-    out = rest[-1]
-    summed = received[0, 2]
-    for number in range(1, 4):
-        summed = summed + received[number, 2]
-    out[0:8, :] = summed[:, 0:64]
-    out[8:16, :] = summed[:, 128:192]
-
-
-def last_kernel(links, inner, *rest):
-    received, solutions, total = rest[:5], rest[5], rest[6]
+    for face, out in zip(faces, faces_out):
+        out[...] = face[...]
+    at = lax.broadcasted_iota(jnp.int32, (128, 64), 0)
+    wanted = jnp.where((at & 7) < 4, (at & 7) << 4 | at >> 3, 64)
+    order = (lax.broadcasted_iota(jnp.int32, (128, 64), 1) == wanted).astype(F32)
+    partial[...] = jnp.zeros_like(partial)
+    partial[:, 0:64] = product(order, projections(eigvecs, inner, psi, carried, first, second), (1, 0))
+
+
+def far_kernel(parts, x_faces, out):
+    out[...] = jnp.zeros_like(out)
+    number = lax.axis_index("space") >> 4
+    out[number ^ 1, 0:2] = x_faces[0]
+    out[number ^ 2, 0:2] = x_faces[1]
+    rows = parts[0]
+    for i in range(1, 16):
+        rows = rows + parts[i]
+    for n in range(4):
+        out[n, 2, 0:1, 0:128] = rows[n : n + 1, :]
+
+
+def last_kernel(scale, links, inner, *rest):
+    received, solutions, reduced, total = rest[:5], rest[5], rest[6], rest[7]
     hop(total, links, None, None, field_halos(received) + [(None, None)])
     for q in range(24):
         solutions[q] = (inner[q] + (RELAXATION[2] * HOPPING) * total[q])[:, 0:SITES]
+    row = received[0][0, 2, 0:1, 0:64]
+    for n in range(1, 4):
+        row = row + received[0][n, 2, 0:1, 0:64]
+    column = lax.broadcasted_iota(jnp.int32, (8, 64), 1)
+    spread = jnp.where(column >> 3 == lax.broadcasted_iota(jnp.int32, (8, 64), 0), row * scale, 0.0)
+    entry = lax.broadcasted_iota(jnp.int32, (64, 8), 0) & 7
+    reduced[...] = product(spread, (entry == lax.broadcasted_iota(jnp.int32, (64, 8), 1)).astype(F32), (1, 0))
 
 
 def call(kernel, outs, args, scratch=(), place=pltpu.VMEM):
@@ -558,26 +573,31 @@
         [FIELD],
     )
     second, slices = exchanged(sends, (ahead, behind))
-    psi, carried, inner, ahead, behind = call(
+    psi, carried, inner, ahead, behind, x_faces, *faces = call(
         second_kernel,
-        [FIELD, CARRIED, FIELD] + SLICES,
+        [FIELD, CARRIED, FIELD] + SLICES + [(2, 2, 8, LANES)] + faces_of(2)[2:],
         (dilution, chosen, links, packed, psi, carried, *second, *slices),
         [FIELD],
     )
     slices = shifted((ahead, behind))
-    inner, *sends = call(
+    y_far = flipped(faces[1], 3)
+    inner, partial, *faces = call(
         project_kernel,
-        [FIELD, (4, 3, 8, LANES)] + faces_of(2)[2:],
-        (links, eigvecs, psi, carried, inner, *slices, *first, *second),
+        [FIELD, (128, 128)] + faces_of(2)[:3],
+        (links, eigvecs, psi, carried, inner, *slices, *first, *second, faces[0], faces[2], faces[3]),
         [FIELD],
     )
-    third = [on_line(sends[0])] + [flipped(send, n + 2) for n, send in enumerate(sends[1:])]
-    (rows,) = call(line_sum_kernel, [(16, 64)], third)
     blocks = [[16 * n + i for i in range(16)] for n in range(4)]
-    parts = lax.all_to_all(rows, "space", 0, 0, axis_index_groups=blocks, tiled=True)
-    volume = SITES * lax.axis_size("space")
-    reduced = jnp.sum(parts, axis=0) * (1.0 / (3.0 * volume))
-    (solutions,) = call(last_kernel, [(24, 8, SITES)], (links, inner, *third), [FIELD])
+    parts = lax.all_to_all(
+        partial.reshape(16, 8, 128), "space", 0, 0, axis_index_groups=blocks, tiled=True
+    )
+    near = [flipped(face, n) for face, n in zip(faces, (2, 4, 5))]
+    (far,) = call(far_kernel, [(4, 3, 8, LANES)], (parts, x_faces))
+    third = [on_line(far), near[0], y_far, near[1], near[2]]
+    scale = 1.0 / (3.0 * SITES * lax.axis_size("space"))
+    solutions, reduced = call(
+        functools.partial(last_kernel, scale), [(24, 8, SITES), (8, 8)], (links, inner, *third), [FIELD]
+    )
     return solutions.reshape(2, 4, 3, 1, 8, SITES), reduced.reshape(1, 1, 2, 4, 8)
 
 

time: 181 us -> 183 us (1.011)
  blocking collectives: 0 us -> 20.4 us
  starting transfers between devices: 135 us -> 123 us
  waiting for transfers between devices: 33.5 us -> 27.8 us
    all_to_all x0 -> x1, blocking collectives: none -> 20.4 us  [body(): lax.all_to_all(partial.reshape(16, 8, 128), 'space', 0, 0, axis_index_gro...]
    all_to_all x1 -> x0, waiting for transfers between devices: 10.4 us -> none  [body(): lax.all_to_all(rows, 'space', 0, 0, axis_index_groups=blocks, tiled=True)]
    all_to_all x1 -> x0, starting transfers between devices: 5.74 us -> none  [body(): lax.all_to_all(rows, 'space', 0, 0, axis_index_groups=blocks, tiled=True)]
    all_to_all x1, waiting for transfers between devices: 8.76 us -> 12.4 us  [on_line(): lax.all_to_all(value, 'space', 0, 0, axis_index_groups=lines, tiled=True)]
    ppermute x16, starting transfers between devices: 101 us -> 98.2 us  [flipped(): lax.ppermute(value, 'space', [(i, i ^ 1 << BITS[n]) for i in range(lax.ax...]
    all_to_all x1, starting transfers between devices: 12.9 us -> 10.2 us  [on_line(): lax.all_to_all(value, 'space', 0, 0, axis_index_groups=lines, tiled=True)]
  transfers between devices with their start and end apart: 24 -> 23, of which waited for: 7 -> 7; matrix products, arithmetic and copies ran while one was open for 0% -> 0% of each run, Pallas kernels for 1% -> 0%
where the time goes in v1:
time: 183 us; the launch traced here: 182 us
  starting transfers between devices  123 us (67%)
  waiting for transfers between devices  27.8 us (15%)
  blocking collectives  20.4 us (11%)
  Pallas kernels  6.92 us (4%)
  local copies, waits for them, and re-layouts  2.56 us (1%)
    ppermute x16, starting transfers between devices, flipped(): lax.ppermute(value, 'space', [(i, i ^ 1 << BITS[n]) for i in range(lax.ax...  98.2 us
    all_to_all x1, blocking collectives, body(): lax.all_to_all(partial.reshape(16, 8, 128), 'space', 0, 0, axis_index_gro...  20.4 us
    ppermute x6, starting transfers between devices, shifted(): lax.ppermute(slices[n], 'tm', [(i, (i + by) % length) for i in range(leng...  15 us
    all_to_all x1, waiting for transfers between devices, on_line(): lax.all_to_all(value, 'space', 0, 0, axis_index_groups=lines, tiled=True)  12.4 us
    all_to_all x1, starting transfers between devices, on_line(): lax.all_to_all(value, 'space', 0, 0, axis_index_groups=lines, tiled=True)  10.2 us
    ppermute x16, waiting for transfers between devices, flipped(): lax.ppermute(value, 'space', [(i, i ^ 1 << BITS[n]) for i in range(lax.ax...  9.67 us
    pallas_call x7, Pallas kernels, call(): pl.pallas_call(kernel, out_shape=[jax.ShapeDtypeStruct(shape, F32) for sh...  6.92 us
    ppermute x6, waiting for transfers between devices, shifted(): lax.ppermute(slices[n], 'tm', [(i, (i + by) % length) for i in range(leng...  5.63 us
  transfers between devices with their start and end apart: 23, of which 7 were waited for; matrix products, arithmetic and copies ran while one was open for 0% of the time, Pallas kernels for 0%

profile of v1, /device:TPU:32, one launch (start us, length us, event | category | flops | bytes accessed | tf_op | source)
XLA Modules:
  0.0 182.0 jit_solution(14611847347675044450)
XLA Ops:
  0.6 0.0 copy-start.4
  0.6 0.7 copy-done.4
  1.3 0.0 copy-start
  1.3 1.0 copy-done
  2.3 0.0 copy-start.3
  2.3 0.9 copy-done.3
  3.2 0.0 copy-start.2
  3.2 1.4 shard_map.59
  4.6 15.7 %collective-permute-start = (f32[5,8,256]{2,1,0:T(8,128)S(1)}, f32[5,8,256]{2,1,0:T(8,128)S(1)}, u32[]{:S(2)}, u32[]{:S(2)}) collective-permute-start(f32[5,8,256]{2,1,0:T(8,128)S(1)} %get-tuple-element.45), channel_id=1, source_target_pairs={{0,16},{1,17},{2,18},{3,19},{4,20},{5,21},{6,22},{7,23},{8,24},{9,... | collective-permute-start | bytes 122888 | tf_op jit(solution)/shard_map/ppermute | solution.py:532
  20.3 18.5 %collective-permute-start.1 = (f32[5,8,256]{2,1,0:T(8,128)S(1)}, f32[5,8,256]{2,1,0:T(8,128)S(1)}, u32[]{:S(2)}, u32[]{:S(2)}) collective-permute-start(f32[5,8,256]{2,1,0:T(8,128)S(1)} %get-tuple-element.46), channel_id=1, source_target_pairs={{0,32},{1,33},{2,34},{3,35},{4,36},{5,37},{6,38},{7,39},{8,40},{9,... | collective-permute-start | bytes 122888 | tf_op jit(solution)/shard_map/ppermute | solution.py:532
  38.8 3.4 %collective-permute-start.2 = (f32[5,8,256]{2,1,0:T(8,128)S(1)}, f32[5,8,256]{2,1,0:T(8,128)S(1)}, u32[]{:S(2)}, u32[]{:S(2)}) collective-permute-start(f32[5,8,256]{2,1,0:T(8,128)S(1)} %get-tuple-element.47), channel_id=1, source_target_pairs={{0,4},{1,5},{2,6},{3,7},{4,0},{5,1},{6,2},{7,3},{8,12},{9,13},{10,... | collective-permute-start | bytes 122888 | tf_op jit(solution)/shard_map/ppermute | solution.py:532
  42.2 4.4 %collective-permute-start.6 = (f32[6,8,256]{2,1,0:T(8,128)S(1)}, f32[6,8,256]{2,1,0:T(8,128)S(1)}, u32[]{:S(2)}, u32[]{:S(2)}) collective-permute-start(f32[6,8,256]{2,1,0:T(8,128)S(1)} %get-tuple-element.51), channel_id=1, source_target_pairs={{0,960},{64,0},{128,64},{192,128},{256,192},{320,256},{384,320},{4... | collective-permute-start | bytes 147464 | tf_op jit(solution)/shard_map/ppermute | solution.py:544
  46.6 1.9 %collective-permute-start.7 = (f32[6,8,256]{2,1,0:T(8,128)S(1)}, f32[6,8,256]{2,1,0:T(8,128)S(1)}, u32[]{:S(2)}, u32[]{:S(2)}) collective-permute-start(f32[6,8,256]{2,1,0:T(8,128)S(1)} %get-tuple-element.52), channel_id=1, source_target_pairs={{0,64},{64,128},{128,192},{192,256},{256,320},{320,384},{384,448},... | collective-permute-start | bytes 147464 | tf_op jit(solution)/shard_map/ppermute | solution.py:544
  48.6 0.0 collective-permute-done.rest_0_.rest_2_
  48.6 4.3 %collective-permute-start.3 = (f32[5,8,256]{2,1,0:T(8,128)S(1)}, f32[5,8,256]{2,1,0:T(8,128)S(1)}, u32[]{:S(2)}, u32[]{:S(2)}) collective-permute-start(f32[5,8,256]{2,1,0:T(8,128)S(1)} %get-tuple-element.48), channel_id=1, source_target_pairs={{0,8},{1,9},{2,10},{3,11},{4,12},{5,13},{6,14},{7,15},{8,0},{9,1},... | collective-permute-start | bytes 122888 | tf_op jit(solution)/shard_map/ppermute | solution.py:532
  52.9 0.0 collective-permute-done.1.rest_1_.rest_3_
  52.9 4.6 %collective-permute-start.4 = (f32[5,8,256]{2,1,0:T(8,128)S(1)}, f32[5,8,256]{2,1,0:T(8,128)S(1)}, u32[]{:S(2)}, u32[]{:S(2)}) collective-permute-start(f32[5,8,256]{2,1,0:T(8,128)S(1)} %get-tuple-element.49), channel_id=1, source_target_pairs={{0,1},{1,0},{2,3},{3,2},{4,5},{5,4},{6,7},{7,6},{8,9},{9,8},{10,11... | collective-permute-start | bytes 122888 | tf_op jit(solution)/shard_map/ppermute | solution.py:532
  57.5 0.0 collective-permute-done.2.rest_2_.rest_4_
  57.5 2.9 %collective-permute-start.5 = (f32[5,8,256]{2,1,0:T(8,128)S(1)}, f32[5,8,256]{2,1,0:T(8,128)S(1)}, u32[]{:S(2)}, u32[]{:S(2)}) collective-permute-start(f32[5,8,256]{2,1,0:T(8,128)S(1)} %get-tuple-element.50), channel_id=1, source_target_pairs={{0,2},{1,3},{2,0},{3,1},{4,6},{5,7},{6,4},{7,5},{8,10},{9,11},{10,... | collective-permute-start | bytes 122888 | tf_op jit(solution)/shard_map/ppermute | solution.py:532
  60.5 0.0 copy-done.2
  60.5 0.1 shard_map.60.clover
  60.5 0.0 collective-permute-done.3.rest_3_.rest_5_
  60.6 0.0 collective-permute-done.4.rest_4_.rest_6_
  60.6 2.9 %collective-permute-done.5.rest_5_.rest_7_ = f32[5,8,256]{2,1,0:T(8,128)S(1)} collective-permute-done((f32[5,8,256]{2,1,0:T(8,128)S(1)}, f32[5,8,256]{2,1,0:T(8,128)S(1)}, u32[]{:S(2)}, u32[]{:S(2)}) %collective-permute-start.5) | collective-permute-done | bytes 40992 | tf_op jit(solution)/shard_map/ppermute | solution.py:532
  63.4 0.0 collective-permute-done.6.rest_6_
  63.4 0.0 collective-permute-done.7.rest_7_
  63.4 1.0 shard_map.61
  64.5 8.4 %collective-permute-start.8 = (f32[6,8,256]{2,1,0:T(8,128)S(1)}, f32[6,8,256]{2,1,0:T(8,128)S(1)}, u32[]{:S(2)}, u32[]{:S(2)}) collective-permute-start(f32[6,8,256]{2,1,0:T(8,128)S(1)} %get-tuple-element.55), channel_id=1, source_target_pairs={{0,16},{1,17},{2,18},{3,19},{4,20},{5,21},{6,22},{7,23},{8,24},{9,... | collective-permute-start | bytes 147464 | tf_op jit(solution)/shard_map/ppermute | solution.py:532
  72.9 13.6 %collective-permute-start.9 = (f32[6,8,256]{2,1,0:T(8,128)S(1)}, f32[6,8,256]{2,1,0:T(8,128)S(1)}, u32[]{:S(2)}, u32[]{:S(2)}) collective-permute-start(f32[6,8,256]{2,1,0:T(8,128)S(1)} %get-tuple-element.56), channel_id=1, source_target_pairs={{0,32},{1,33},{2,34},{3,35},{4,36},{5,37},{6,38},{7,39},{8,40},{9,... | collective-permute-start | bytes 147464 | tf_op jit(solution)/shard_map/ppermute | solution.py:532
  86.5 1.9 %collective-permute-start.10 = (f32[6,8,256]{2,1,0:T(8,128)S(1)}, f32[6,8,256]{2,1,0:T(8,128)S(1)}, u32[]{:S(2)}, u32[]{:S(2)}) collective-permute-start(f32[6,8,256]{2,1,0:T(8,128)S(1)} %get-tuple-element.57), channel_id=1, source_target_pairs={{0,4},{1,5},{2,6},{3,7},{4,0},{5,1},{6,2},{7,3},{8,12},{9,13},{10,... | collective-permute-start | bytes 147464 | tf_op jit(solution)/shard_map/ppermute | solution.py:532
  88.4 1.9 %collective-permute-start.14 = (f32[12,8,256]{2,1,0:T(8,128)S(1)}, f32[12,8,256]{2,1,0:T(8,128)S(1)}, u32[]{:S(2)}, u32[]{:S(2)}) collective-permute-start(f32[12,8,256]{2,1,0:T(8,128)S(1)} %get-tuple-element.61), channel_id=1, source_target_pairs={{0,960},{64,0},{128,64},{192,128},{256,192},{320,256},{384,320},{4... | collective-permute-start | bytes 294920 | tf_op jit(solution)/shard_map/ppermute | solution.py:544
  90.3 2.4 %collective-permute-start.15 = (f32[12,8,256]{2,1,0:T(8,128)S(1)}, f32[12,8,256]{2,1,0:T(8,128)S(1)}, u32[]{:S(2)}, u32[]{:S(2)}) collective-permute-start(f32[12,8,256]{2,1,0:T(8,128)S(1)} %get-tuple-element.62), channel_id=1, source_target_pairs={{0,64},{64,128},{128,192},{192,256},{256,320},{320,384},{384,448},... | collective-permute-start | bytes 294920 | tf_op jit(solution)/shard_map/ppermute | solution.py:544
  92.8 0.0 collective-permute-done.8.rest_0_.rest_8_
  92.8 4.7 %collective-permute-start.11 = (f32[6,8,256]{2,1,0:T(8,128)S(1)}, f32[6,8,256]{2,1,0:T(8,128)S(1)}, u32[]{:S(2)}, u32[]{:S(2)}) collective-permute-start(f32[6,8,256]{2,1,0:T(8,128)S(1)} %get-tuple-element.58), channel_id=1, source_target_pairs={{0,8},{1,9},{2,10},{3,11},{4,12},{5,13},{6,14},{7,15},{8,0},{9,1},... | collective-permute-start | bytes 147464 | tf_op jit(solution)/shard_map/ppermute | solution.py:532
  97.4 1.8 collective-permute-done.9.rest_1_.rest_9_
  99.2 2.7 %collective-permute-start.12 = (f32[6,8,256]{2,1,0:T(8,128)S(1)}, f32[6,8,256]{2,1,0:T(8,128)S(1)}, u32[]{:S(2)}, u32[]{:S(2)}) collective-permute-start(f32[6,8,256]{2,1,0:T(8,128)S(1)} %get-tuple-element.59), channel_id=1, source_target_pairs={{0,1},{1,0},{2,3},{3,2},{4,5},{5,4},{6,7},{7,6},{8,9},{9,8},{10,11... | collective-permute-start | bytes 147464 | tf_op jit(solution)/shard_map/ppermute | solution.py:532
  101.9 0.0 collective-permute-done.10.rest_2_.rest_10_
  101.9 6.5 %collective-permute-start.13 = (f32[6,8,256]{2,1,0:T(8,128)S(1)}, f32[6,8,256]{2,1,0:T(8,128)S(1)}, u32[]{:S(2)}, u32[]{:S(2)}) collective-permute-start(f32[6,8,256]{2,1,0:T(8,128)S(1)} %get-tuple-element.60), channel_id=1, source_target_pairs={{0,2},{1,3},{2,0},{3,1},{4,6},{5,7},{6,4},{7,5},{8,10},{9,11},{10,... | collective-permute-start | bytes 147464 | tf_op jit(solution)/shard_map/ppermute | solution.py:532
  108.4 0.0 collective-permute-done.11.rest_3_.rest_11_
  108.4 0.0 collective-permute-done.12.rest_4_.rest_12_
  108.4 2.0 %collective-permute-done.13.rest_5_.rest_13_ = f32[6,8,256]{2,1,0:T(8,128)S(1)} collective-permute-done((f32[6,8,256]{2,1,0:T(8,128)S(1)}, f32[6,8,256]{2,1,0:T(8,128)S(1)}, u32[]{:S(2)}, u32[]{:S(2)}) %collective-permute-start.13) | collective-permute-done | bytes 49184 | tf_op jit(solution)/shard_map/ppermute | solution.py:532
  110.4 0.0 collective-permute-done.14.rest_6_
  110.4 0.0 collective-permute-done.15.rest_7_
  110.4 0.0 copy-start.1
  110.4 1.5 shard_map.62
  112.0 1.9 %collective-permute-start.16 = (f32[12,8,256]{2,1,0:T(8,128)S(1)}, f32[12,8,256]{2,1,0:T(8,128)S(1)}, u32[]{:S(2)}, u32[]{:S(2)}) collective-permute-start(f32[12,8,256]{2,1,0:T(8,128)S(1)} %get-tuple-element.66), channel_id=1, source_target_pairs={{0,960},{64,0},{128,64},{192,128},{256,192},{320,256},{384,320},{4... | collective-permute-start | bytes 294920 | tf_op jit(solution)/shard_map/ppermute | solution.py:544
  113.9 2.4 %collective-permute-start.17 = (f32[12,8,256]{2,1,0:T(8,128)S(1)}, f32[12,8,256]{2,1,0:T(8,128)S(1)}, u32[]{:S(2)}, u32[]{:S(2)}) collective-permute-start(f32[12,8,256]{2,1,0:T(8,128)S(1)} %get-tuple-element.67), channel_id=1, source_target_pairs={{0,64},{64,128},{128,192},{192,256},{256,320},{320,384},{384,448},... | collective-permute-start | bytes 294920 | tf_op jit(solution)/shard_map/ppermute | solution.py:544
  116.3 0.0 collective-permute-done.16.rest_0_
  116.3 5.6 %collective-permute-done.17.rest_1_ = f32[12,8,256]{2,1,0:T(8,128)S(1)} collective-permute-done((f32[12,8,256]{2,1,0:T(8,128)S(1)}, f32[12,8,256]{2,1,0:T(8,128)S(1)}, u32[]{:S(2)}, u32[]{:S(2)}) %collective-permute-start.17) | collective-permute-done | bytes 98336 | tf_op jit(solution)/shard_map/ppermute | solution.py:544
  122.0 0.0 copy-done.1
  122.0 1.3 shard_map.63
  123.3 20.4 %all_to_all.10.parts = f32[16,8,128]{2,1,0:T(8,128)S(1)} all-to-all(f32[16,8,128]{2,1,0:T(8,128)S(1)} %bitcast.17), channel_id=1, replica_groups={{0,1,2,3,4,5,6,7,8,9,10,11,12,13,14,15},{16,17,18,19,20,21,22,23,24,25,..., dimensions={0} | all-to-all | bytes 131072 | tf_op jit(solution)/shard_map/all_to_all | solution.py:591
  143.7 0.7 shard_map.64
  144.4 10.2 %all-to-all-start.1 = ((f32[4,3,8,256]{3,2,1,0:T(8,128)}), f32[4,3,8,256]{3,2,1,0:T(8,128)S(1)}, u32[]{:S(2)}, u32[]{:S(2)}) async-start(f32[4,3,8,256]{3,2,1,0:T(8,128)} %shard_map.64), calls=%async_computation.1 | async-start | bytes 196608 | tf_op jit(solution)/shard_map/all_to_all | solution.py:537
  154.6 2.6 %collective-permute-start.19 = (f32[2,8,256]{2,1,0:T(8,128)S(1)}, f32[2,8,256]{2,1,0:T(8,128)S(1)}, u32[]{:S(2)}, u32[]{:S(2)}) collective-permute-start(f32[2,8,256]{2,1,0:T(8,128)S(1)} %get-tuple-element.75), channel_id=1, source_target_pairs={{0,8},{1,9},{2,10},{3,11},{4,12},{5,13},{6,14},{7,15},{8,0},{9,1},... | collective-permute-start | bytes 49160 | tf_op jit(solution)/shard_map/ppermute | solution.py:532
  157.2 3.3 %collective-permute-start.18 = (f32[2,8,256]{2,1,0:T(8,128)S(1)}, f32[2,8,256]{2,1,0:T(8,128)S(1)}, u32[]{:S(2)}, u32[]{:S(2)}) collective-permute-start(f32[2,8,256]{2,1,0:T(8,128)S(1)} %get-tuple-element.74), channel_id=1, source_target_pairs={{0,4},{1,5},{2,6},{3,7},{4,0},{5,1},{6,2},{7,3},{8,12},{9,13},{10,... | collective-permute-start | bytes 49160 | tf_op jit(solution)/shard_map/ppermute | solution.py:532
  160.5 2.2 %collective-permute-start.20 = (f32[2,8,256]{2,1,0:T(8,128)S(1)}, f32[2,8,256]{2,1,0:T(8,128)S(1)}, u32[]{:S(2)}, u32[]{:S(2)}) collective-permute-start(f32[2,8,256]{2,1,0:T(8,128)S(1)} %get-tuple-element.76), channel_id=1, source_target_pairs={{0,1},{1,0},{2,3},{3,2},{4,5},{5,4},{6,7},{7,6},{8,9},{9,8},{10,11... | collective-permute-start | bytes 49160 | tf_op jit(solution)/shard_map/ppermute | solution.py:532
  162.7 2.9 %collective-permute-start.21 = (f32[2,8,256]{2,1,0:T(8,128)S(1)}, f32[2,8,256]{2,1,0:T(8,128)S(1)}, u32[]{:S(2)}, u32[]{:S(2)}) collective-permute-start(f32[2,8,256]{2,1,0:T(8,128)S(1)} %get-tuple-element.77), channel_id=1, source_target_pairs={{0,2},{1,3},{2,0},{3,1},{4,6},{5,7},{6,4},{7,5},{8,10},{9,11},{10,... | collective-permute-start | bytes 49160 | tf_op jit(solution)/shard_map/ppermute | solution.py:532
  165.6 0.0 collective-permute-done.19.rest_2_
  165.6 0.0 collective-permute-done.18.rest_1_
  165.6 2.0 %collective-permute-done.20.rest_3_ = f32[2,8,256]{2,1,0:T(8,128)S(1)} collective-permute-done((f32[2,8,256]{2,1,0:T(8,128)S(1)}, f32[2,8,256]{2,1,0:T(8,128)S(1)}, u32[]{:S(2)}, u32[]{:S(2)}) %collective-permute-start.20) | collective-permute-done | bytes 16416 | tf_op jit(solution)/shard_map/ppermute | solution.py:532
  167.7 0.9 collective-permute-done.21.rest_4_
  168.6 12.4 %all-to-all-done.1.rest_0_ = f32[4,3,8,256]{3,2,1,0:T(8,128)S(1)} async-done(((f32[4,3,8,256]{3,2,1,0:T(8,128)}), f32[4,3,8,256]{3,2,1,0:T(8,128)S(1)}, u32[]{:S(2)}, u32[]{:S(2)}) %all-to-all-start.1) | async-done | bytes 98336 | tf_op jit(solution)/shard_map/all_to_all | solution.py:537
  181.1 1.0 shard_map.65
Async XLA Ops:
  0.6 0.7 copy-start.4
  1.3 1.0 copy-start
  2.3 0.9 copy-start.3
  3.2 57.3 %copy-start.2 = (f32[1,2,2,6,6,216]{5,2,4,3,1,0:T(2,128)S(1)}, f32[1,2,2,6,6,216]{5,2,4,3,1,0:T(2,128)}, u32[]{:S(2)}) copy-start(f32[1,2,2,6,6,216]{5,2,4,3,1,0:T(2,128)} %param.7) | copy-start | bytes 373252
  4.6 44.0 %collective-permute-start = (f32[5,8,256]{2,1,0:T(8,128)S(1)}, f32[5,8,256]{2,1,0:T(8,128)S(1)}, u32[]{:S(2)}, u32[]{:S(2)}) collective-permute-start(f32[5,8,256]{2,1,0:T(8,128)S(1)} %get-tuple-element.45), channel_id=1, source_target_pairs={{0,16},{1,17},{2,18},{3,19},{4,20},{5,21},{6,22},{7,23},{8,24},{9,... | collective-permute-start | bytes 122888 | tf_op jit(solution)/shard_map/ppermute | solution.py:532
  20.3 32.6 %collective-permute-start.1 = (f32[5,8,256]{2,1,0:T(8,128)S(1)}, f32[5,8,256]{2,1,0:T(8,128)S(1)}, u32[]{:S(2)}, u32[]{:S(2)}) collective-permute-start(f32[5,8,256]{2,1,0:T(8,128)S(1)} %get-tuple-element.46), channel_id=1, source_target_pairs={{0,32},{1,33},{2,34},{3,35},{4,36},{5,37},{6,38},{7,39},{8,40},{9,... | collective-permute-start | bytes 122888 | tf_op jit(solution)/shard_map/ppermute | solution.py:532
  38.8 18.7 %collective-permute-start.2 = (f32[5,8,256]{2,1,0:T(8,128)S(1)}, f32[5,8,256]{2,1,0:T(8,128)S(1)}, u32[]{:S(2)}, u32[]{:S(2)}) collective-permute-start(f32[5,8,256]{2,1,0:T(8,128)S(1)} %get-tuple-element.47), channel_id=1, source_target_pairs={{0,4},{1,5},{2,6},{3,7},{4,0},{5,1},{6,2},{7,3},{8,12},{9,13},{10,... | collective-permute-start | bytes 122888 | tf_op jit(solution)/shard_map/ppermute | solution.py:532
  42.2 21.3 %collective-permute-start.6 = (f32[6,8,256]{2,1,0:T(8,128)S(1)}, f32[6,8,256]{2,1,0:T(8,128)S(1)}, u32[]{:S(2)}, u32[]{:S(2)}) collective-permute-start(f32[6,8,256]{2,1,0:T(8,128)S(1)} %get-tuple-element.51), channel_id=1, source_target_pairs={{0,960},{64,0},{128,64},{192,128},{256,192},{320,256},{384,320},{4... | collective-permute-start | bytes 147464 | tf_op jit(solution)/shard_map/ppermute | solution.py:544
  46.6 16.8 %collective-permute-start.7 = (f32[6,8,256]{2,1,0:T(8,128)S(1)}, f32[6,8,256]{2,1,0:T(8,128)S(1)}, u32[]{:S(2)}, u32[]{:S(2)}) collective-permute-start(f32[6,8,256]{2,1,0:T(8,128)S(1)} %get-tuple-element.52), channel_id=1, source_target_pairs={{0,64},{64,128},{128,192},{192,256},{256,320},{320,384},{384,448},... | collective-permute-start | bytes 147464 | tf_op jit(solution)/shard_map/ppermute | solution.py:544
  48.6 12.0 %collective-permute-start.3 = (f32[5,8,256]{2,1,0:T(8,128)S(1)}, f32[5,8,256]{2,1,0:T(8,128)S(1)}, u32[]{:S(2)}, u32[]{:S(2)}) collective-permute-start(f32[5,8,256]{2,1,0:T(8,128)S(1)} %get-tuple-element.48), channel_id=1, source_target_pairs={{0,8},{1,9},{2,10},{3,11},{4,12},{5,13},{6,14},{7,15},{8,0},{9,1},... | collective-permute-start | bytes 122888 | tf_op jit(solution)/shard_map/ppermute | solution.py:532
  52.9 7.7 %collective-permute-start.4 = (f32[5,8,256]{2,1,0:T(8,128)S(1)}, f32[5,8,256]{2,1,0:T(8,128)S(1)}, u32[]{:S(2)}, u32[]{:S(2)}) collective-permute-start(f32[5,8,256]{2,1,0:T(8,128)S(1)} %get-tuple-element.49), channel_id=1, source_target_pairs={{0,1},{1,0},{2,3},{3,2},{4,5},{5,4},{6,7},{7,6},{8,9},{9,8},{10,11... | collective-permute-start | bytes 122888 | tf_op jit(solution)/shard_map/ppermute | solution.py:532
  57.5 5.9 %collective-permute-start.5 = (f32[5,8,256]{2,1,0:T(8,128)S(1)}, f32[5,8,256]{2,1,0:T(8,128)S(1)}, u32[]{:S(2)}, u32[]{:S(2)}) collective-permute-start(f32[5,8,256]{2,1,0:T(8,128)S(1)} %get-tuple-element.50), channel_id=1, source_target_pairs={{0,2},{1,3},{2,0},{3,1},{4,6},{5,7},{6,4},{7,5},{8,10},{9,11},{10,... | collective-permute-start | bytes 122888 | tf_op jit(solution)/shard_map/ppermute | solution.py:532
  64.5 28.3 %collective-permute-start.8 = (f32[6,8,256]{2,1,0:T(8,128)S(1)}, f32[6,8,256]{2,1,0:T(8,128)S(1)}, u32[]{:S(2)}, u32[]{:S(2)}) collective-permute-start(f32[6,8,256]{2,1,0:T(8,128)S(1)} %get-tuple-element.55), channel_id=1, source_target_pairs={{0,16},{1,17},{2,18},{3,19},{4,20},{5,21},{6,22},{7,23},{8,24},{9,... | collective-permute-start | bytes 147464 | tf_op jit(solution)/shard_map/ppermute | solution.py:532
  72.9 26.3 %collective-permute-start.9 = (f32[6,8,256]{2,1,0:T(8,128)S(1)}, f32[6,8,256]{2,1,0:T(8,128)S(1)}, u32[]{:S(2)}, u32[]{:S(2)}) collective-permute-start(f32[6,8,256]{2,1,0:T(8,128)S(1)} %get-tuple-element.56), channel_id=1, source_target_pairs={{0,32},{1,33},{2,34},{3,35},{4,36},{5,37},{6,38},{7,39},{8,40},{9,... | collective-permute-start | bytes 147464 | tf_op jit(solution)/shard_map/ppermute | solution.py:532
  86.5 15.4 %collective-permute-start.10 = (f32[6,8,256]{2,1,0:T(8,128)S(1)}, f32[6,8,256]{2,1,0:T(8,128)S(1)}, u32[]{:S(2)}, u32[]{:S(2)}) collective-permute-start(f32[6,8,256]{2,1,0:T(8,128)S(1)} %get-tuple-element.57), channel_id=1, source_target_pairs={{0,4},{1,5},{2,6},{3,7},{4,0},{5,1},{6,2},{7,3},{8,12},{9,13},{10,... | collective-permute-start | bytes 147464 | tf_op jit(solution)/shard_map/ppermute | solution.py:532
  88.4 22.0 %collective-permute-start.14 = (f32[12,8,256]{2,1,0:T(8,128)S(1)}, f32[12,8,256]{2,1,0:T(8,128)S(1)}, u32[]{:S(2)}, u32[]{:S(2)}) collective-permute-start(f32[12,8,256]{2,1,0:T(8,128)S(1)} %get-tuple-element.61), channel_id=1, source_target_pairs={{0,960},{64,0},{128,64},{192,128},{256,192},{320,256},{384,320},{4... | collective-permute-start | bytes 294920 | tf_op jit(solution)/shard_map/ppermute | solution.py:544
  90.3 20.1 %collective-permute-start.15 = (f32[12,8,256]{2,1,0:T(8,128)S(1)}, f32[12,8,256]{2,1,0:T(8,128)S(1)}, u32[]{:S(2)}, u32[]{:S(2)}) collective-permute-start(f32[12,8,256]{2,1,0:T(8,128)S(1)} %get-tuple-element.62), channel_id=1, source_target_pairs={{0,64},{64,128},{128,192},{192,256},{256,320},{320,384},{384,448},... | collective-permute-start | bytes 294920 | tf_op jit(solution)/shard_map/ppermute | solution.py:544
  92.8 15.6 %collective-permute-start.11 = (f32[6,8,256]{2,1,0:T(8,128)S(1)}, f32[6,8,256]{2,1,0:T(8,128)S(1)}, u32[]{:S(2)}, u32[]{:S(2)}) collective-permute-start(f32[6,8,256]{2,1,0:T(8,128)S(1)} %get-tuple-element.58), channel_id=1, source_target_pairs={{0,8},{1,9},{2,10},{3,11},{4,12},{5,13},{6,14},{7,15},{8,0},{9,1},... | collective-permute-start | bytes 147464 | tf_op jit(solution)/shard_map/ppermute | solution.py:532
  99.2 9.2 %collective-permute-start.12 = (f32[6,8,256]{2,1,0:T(8,128)S(1)}, f32[6,8,256]{2,1,0:T(8,128)S(1)}, u32[]{:S(2)}, u32[]{:S(2)}) collective-permute-start(f32[6,8,256]{2,1,0:T(8,128)S(1)} %get-tuple-element.59), channel_id=1, source_target_pairs={{0,1},{1,0},{2,3},{3,2},{4,5},{5,4},{6,7},{7,6},{8,9},{9,8},{10,11... | collective-permute-start | bytes 147464 | tf_op jit(solution)/shard_map/ppermute | solution.py:532
  101.9 8.5 %collective-permute-start.13 = (f32[6,8,256]{2,1,0:T(8,128)S(1)}, f32[6,8,256]{2,1,0:T(8,128)S(1)}, u32[]{:S(2)}, u32[]{:S(2)}) collective-permute-start(f32[6,8,256]{2,1,0:T(8,128)S(1)} %get-tuple-element.60), channel_id=1, source_target_pairs={{0,2},{1,3},{2,0},{3,1},{4,6},{5,7},{6,4},{7,5},{8,10},{9,11},{10,... | collective-permute-start | bytes 147464 | tf_op jit(solution)/shard_map/ppermute | solution.py:532
  110.4 11.5 %copy-start.1 = (f32[2,3,1,64,216]{4,3,2,1,0:T(8,128)S(1)}, f32[2,3,1,64,216]{4,3,2,1,0:T(8,128)}, u32[]{:S(2)}) copy-start(f32[2,3,1,64,216]{4,3,2,1,0:T(8,128)} %param.5) | copy-start | bytes 995332
  112.0 4.3 %collective-permute-start.16 = (f32[12,8,256]{2,1,0:T(8,128)S(1)}, f32[12,8,256]{2,1,0:T(8,128)S(1)}, u32[]{:S(2)}, u32[]{:S(2)}) collective-permute-start(f32[12,8,256]{2,1,0:T(8,128)S(1)} %get-tuple-element.66), channel_id=1, source_target_pairs={{0,960},{64,0},{128,64},{192,128},{256,192},{320,256},{384,320},{4... | collective-permute-start | bytes 294920 | tf_op jit(solution)/shard_map/ppermute | solution.py:544
  113.9 8.0 %collective-permute-start.17 = (f32[12,8,256]{2,1,0:T(8,128)S(1)}, f32[12,8,256]{2,1,0:T(8,128)S(1)}, u32[]{:S(2)}, u32[]{:S(2)}) collective-permute-start(f32[12,8,256]{2,1,0:T(8,128)S(1)} %get-tuple-element.67), channel_id=1, source_target_pairs={{0,64},{64,128},{128,192},{192,256},{256,320},{320,384},{384,448},... | collective-permute-start | bytes 294920 | tf_op jit(solution)/shard_map/ppermute | solution.py:544
  144.4 36.7 %all-to-all-start.1 = ((f32[4,3,8,256]{3,2,1,0:T(8,128)}), f32[4,3,8,256]{3,2,1,0:T(8,128)S(1)}, u32[]{:S(2)}, u32[]{:S(2)}) async-start(f32[4,3,8,256]{3,2,1,0:T(8,128)} %shard_map.64), calls=%async_computation.1 | async-start | bytes 196608 | tf_op jit(solution)/shard_map/all_to_all | solution.py:537
  154.6 11.0 %collective-permute-start.19 = (f32[2,8,256]{2,1,0:T(8,128)S(1)}, f32[2,8,256]{2,1,0:T(8,128)S(1)}, u32[]{:S(2)}, u32[]{:S(2)}) collective-permute-start(f32[2,8,256]{2,1,0:T(8,128)S(1)} %get-tuple-element.75), channel_id=1, source_target_pairs={{0,8},{1,9},{2,10},{3,11},{4,12},{5,13},{6,14},{7,15},{8,0},{9,1},... | collective-permute-start | bytes 49160 | tf_op jit(solution)/shard_map/ppermute | solution.py:532
  157.2 8.4 %collective-permute-start.18 = (f32[2,8,256]{2,1,0:T(8,128)S(1)}, f32[2,8,256]{2,1,0:T(8,128)S(1)}, u32[]{:S(2)}, u32[]{:S(2)}) collective-permute-start(f32[2,8,256]{2,1,0:T(8,128)S(1)} %get-tuple-element.74), channel_id=1, source_target_pairs={{0,4},{1,5},{2,6},{3,7},{4,0},{5,1},{6,2},{7,3},{8,12},{9,13},{10,... | collective-permute-start | bytes 49160 | tf_op jit(solution)/shard_map/ppermute | solution.py:532
  160.5 7.1 %collective-permute-start.20 = (f32[2,8,256]{2,1,0:T(8,128)S(1)}, f32[2,8,256]{2,1,0:T(8,128)S(1)}, u32[]{:S(2)}, u32[]{:S(2)}) collective-permute-start(f32[2,8,256]{2,1,0:T(8,128)S(1)} %get-tuple-element.76), channel_id=1, source_target_pairs={{0,1},{1,0},{2,3},{3,2},{4,5},{5,4},{6,7},{7,6},{8,9},{9,8},{10,11... | collective-permute-start | bytes 49160 | tf_op jit(solution)/shard_map/ppermute | solution.py:532
  162.7 5.9 %collective-permute-start.21 = (f32[2,8,256]{2,1,0:T(8,128)S(1)}, f32[2,8,256]{2,1,0:T(8,128)S(1)}, u32[]{:S(2)}, u32[]{:S(2)}) collective-permute-start(f32[2,8,256]{2,1,0:T(8,128)S(1)} %get-tuple-element.77), channel_id=1, source_target_pairs={{0,2},{1,3},{2,0},{3,1},{4,6},{5,7},{6,4},{7,5},{8,10},{9,11},{10,... | collective-permute-start | bytes 49160 | tf_op jit(solution)/shard_map/ppermute | solution.py:532

commit v2 on v0

--- a/solution.py
+++ b/solution.py
@@ -1,3 +1,5 @@
+import functools
+
 import jax
 import jax.numpy as jnp
 from jax import lax
@@ -146,21 +148,12 @@
 
 
 def place(sends, direction, vector, first, second):
-    if direction == 0 and len(sends) == 5:
-        number = lax.axis_index("space") >> 4
-        sends[0][number ^ 1, vector] = first
-        sends[0][number ^ 2, vector] = second
-    else:
-        sends[2 * direction - 6][vector] = first
-        sends[2 * direction - 5][vector] = second
+    sends[2 * direction][vector] = first
+    sends[2 * direction + 1][vector] = second
 
 
 def arrived(received, direction, vector):
-    if direction == 0 and len(received) == 5:
-        number = lax.axis_index("space") >> 4
-        first, second = received[0][number ^ 1, vector], received[0][number ^ 2, vector]
-    else:
-        first, second = received[2 * direction - 6][vector], received[2 * direction - 5][vector]
+    first, second = received[2 * direction][vector], received[2 * direction + 1][vector]
     low_is_ahead = even_bits(direction)
     return jnp.where(low_is_ahead, first, second), jnp.where(low_is_ahead, second, first)
 
@@ -449,44 +442,36 @@
 
 
 def second_kernel(dilution, chosen, links, clover, spinor, carried_in, *rest):
-    received, slices, (psi, carried, inner), next_slices, total = rest[:6], rest[6:8], rest[8:11], rest[11:13], rest[13]
+    received, slices, (psi, carried, inner), next_slices = rest[:6], rest[6:8], rest[8:11], rest[11:13]
+    sends, total = rest[13:19], rest[19]
     source = source_getter(chosen, masks_of(dilution))
     hop(total, links, getter(spinor), carried_in, field_halos(received) + [(slices[0], slices[1])])
     relax(RELAXATION[1], getter(spinor), source, clover, total, psi)
     emit_slices(getter(psi), links, next_slices)
     carry(getter(psi), links, carried)
+    emit_faces(getter(psi), carried, sends)
     hop(total, links, getter(psi), carried, [(None, None)] * 4)
     relax(RELAXATION[2], getter(psi), source, clover, total, inner)
 
 
 def project_kernel(links, eigvecs, psi, carried, inner_in, *rest):
-    slices, first, second, inner, sends, total = rest[:2], rest[2:8], rest[8:14], rest[14], rest[15:20], rest[20]
+    slices, first, second, inner, partial, total = rest[:2], rest[2:8], rest[8:14], rest[14], rest[15], rest[16]
     hop(total, links, None, None, slice_halos(slices))
     for q in range(24):
         inner[q] = inner_in[q] + (RELAXATION[2] * HOPPING) * total[q]
-    sends[0][...] = jnp.zeros_like(sends[0])
-    emit_faces(getter(psi), carried, sends)
-    partial = projections(eigvecs, inner, psi, carried, first, second)
-    for number in range(4):
-        at = 16 * number
-        sends[0][number, 2, :, 0:64] = partial[at : at + 8, :]
-        sends[0][number, 2, :, 128:192] = partial[at + 8 : at + 16, :]
-
-
-def line_sum_kernel(received, *rest):
-    out = rest[-1]
-    summed = received[0, 2]
-    for number in range(1, 4):
-        summed = summed + received[number, 2]
-    out[0:8, :] = summed[:, 0:64]
-    out[8:16, :] = summed[:, 128:192]
-
-
-def last_kernel(links, inner, *rest):
-    received, solutions, total = rest[:5], rest[5], rest[6]
+    partial[...] = projections(eigvecs, inner, psi, carried, first, second)
+
+
+def last_kernel(scale, links, inner, parts, *rest):
+    received, solutions, reduced, total = rest[:6], rest[6], rest[7], rest[8]
     hop(total, links, None, None, field_halos(received) + [(None, None)])
     for q in range(24):
         solutions[q] = (inner[q] + (RELAXATION[2] * HOPPING) * total[q])[:, 0:SITES]
+    row = jnp.sum(parts[...], axis=0, keepdims=True) * scale
+    column = lax.broadcasted_iota(jnp.int32, (8, 64), 1)
+    spread = jnp.where(column >> 3 == lax.broadcasted_iota(jnp.int32, (8, 64), 0), row, 0.0)
+    entry = lax.broadcasted_iota(jnp.int32, (64, 8), 0) & 7
+    reduced[...] = product(spread, (entry == lax.broadcasted_iota(jnp.int32, (64, 8), 1)).astype(F32), (1, 0))
 
 
 def call(kernel, outs, args, scratch=(), place=pltpu.VMEM):
@@ -515,11 +500,6 @@
 
 def flipped(value, n):
     return lax.ppermute(value, "space", [(i, i ^ 1 << BITS[n]) for i in range(lax.axis_size("space"))])
-
-
-def on_line(value):
-    lines = [[i + 16 * n for n in range(4)] for i in range(16)]
-    return lax.all_to_all(value, "space", 0, 0, axis_index_groups=lines, tiled=True)
 
 
 def shifted(slices):
@@ -558,26 +538,21 @@
         [FIELD],
     )
     second, slices = exchanged(sends, (ahead, behind))
-    psi, carried, inner, ahead, behind = call(
+    psi, carried, inner, ahead, behind, *sends = call(
         second_kernel,
-        [FIELD, CARRIED, FIELD] + SLICES,
+        [FIELD, CARRIED, FIELD] + SLICES + faces_of(2),
         (dilution, chosen, links, packed, psi, carried, *second, *slices),
         [FIELD],
     )
-    slices = shifted((ahead, behind))
-    inner, *sends = call(
-        project_kernel,
-        [FIELD, (4, 3, 8, LANES)] + faces_of(2)[2:],
-        (links, eigvecs, psi, carried, inner, *slices, *first, *second),
-        [FIELD],
-    )
-    third = [on_line(sends[0])] + [flipped(send, n + 2) for n, send in enumerate(sends[1:])]
-    (rows,) = call(line_sum_kernel, [(16, 64)], third)
-    blocks = [[16 * n + i for i in range(16)] for n in range(4)]
-    parts = lax.all_to_all(rows, "space", 0, 0, axis_index_groups=blocks, tiled=True)
-    volume = SITES * lax.axis_size("space")
-    reduced = jnp.sum(parts, axis=0) * (1.0 / (3.0 * volume))
-    (solutions,) = call(last_kernel, [(24, 8, SITES)], (links, inner, *third), [FIELD])
+    third, slices = exchanged(sends, (ahead, behind))
+    inner, partial = call(
+        project_kernel, [FIELD, (64, 64)], (links, eigvecs, psi, carried, inner, *slices, *first, *second), [FIELD]
+    )
+    parts = lax.all_to_all(partial, "space", 0, 0, tiled=True)
+    scale = 1.0 / (3.0 * SITES * lax.axis_size("space"))
+    solutions, reduced = call(
+        functools.partial(last_kernel, scale), [(24, 8, SITES), (8, 8)], (links, inner, parts, *third), [FIELD]
+    )
     return solutions.reshape(2, 4, 3, 1, 8, SITES), reduced.reshape(1, 1, 2, 4, 8)
 
 

time: 181 us -> 181 us (level)
  the two profiles are of different devices: /device:TPU:32 before, /device:TPU:64 now
where the time goes in v2:
time: 181 us; the launch traced here: 180 us
  starting transfers between devices  150 us (83%)
  waiting for transfers between devices  20.6 us (11%)
  Pallas kernels  6.63 us (4%)
  local copies, waits for them, and re-layouts  2.56 us (1%)
    ppermute x18, starting transfers between devices, flipped(): lax.ppermute(value, 'space', [(i, i ^ 1 << BITS[n]) for i in range(lax.ax...  118 us
    all_to_all x1, starting transfers between devices, body(): parts = lax.all_to_all(partial, 'space', 0, 0, tiled=True)  16.3 us
    ppermute x6, starting transfers between devices, shifted(): lax.ppermute(slices[n], 'tm', [(i, (i + by) % length) for i in range(leng...  15 us
    ppermute x18, waiting for transfers between devices, flipped(): lax.ppermute(value, 'space', [(i, i ^ 1 << BITS[n]) for i in range(lax.ax...  15 us
    pallas_call x6, Pallas kernels, call(): pl.pallas_call(kernel, out_shape=[jax.ShapeDtypeStruct(shape, F32) for sh...  6.63 us
    ppermute x6, waiting for transfers between devices, shifted(): lax.ppermute(slices[n], 'tm', [(i, (i + by) % length) for i in range(leng...  5.63 us
  transfers between devices with their start and end apart: 25, of which 6 were waited for; matrix products, arithmetic and copies ran while one was open for 0% of the time, Pallas kernels for 0%

profile of v2, /device:TPU:64, one launch (start us, length us, event | category | flops | bytes accessed | tf_op | source)
XLA Modules:
  0.0 180.4 jit_solution(1677306995329218743)
XLA Ops:
  0.6 0.0 copy-start.4
  0.6 0.7 copy-done.4
  1.3 0.0 copy-start
  1.3 1.0 copy-done
  2.3 0.0 copy-start.3
  2.3 0.9 copy-done.3
  3.2 1.4 shard_map.59
  4.6 15.7 %collective-permute-start = (f32[5,8,256]{2,1,0:T(8,128)S(1)}, f32[5,8,256]{2,1,0:T(8,128)S(1)}, u32[]{:S(2)}, u32[]{:S(2)}) collective-permute-start(f32[5,8,256]{2,1,0:T(8,128)S(1)} %get-tuple-element.43), channel_id=1, source_target_pairs={{0,16},{1,17},{2,18},{3,19},{4,20},{5,21},{6,22},{7,23},{8,24},{9,... | collective-permute-start | bytes 122888 | tf_op jit(solution)/shard_map/ppermute | solution.py:502
  20.3 17.6 %collective-permute-start.1 = (f32[5,8,256]{2,1,0:T(8,128)S(1)}, f32[5,8,256]{2,1,0:T(8,128)S(1)}, u32[]{:S(2)}, u32[]{:S(2)}) collective-permute-start(f32[5,8,256]{2,1,0:T(8,128)S(1)} %get-tuple-element.44), channel_id=1, source_target_pairs={{0,32},{1,33},{2,34},{3,35},{4,36},{5,37},{6,38},{7,39},{8,40},{9,... | collective-permute-start | bytes 122888 | tf_op jit(solution)/shard_map/ppermute | solution.py:502
  37.9 3.4 %collective-permute-start.2 = (f32[5,8,256]{2,1,0:T(8,128)S(1)}, f32[5,8,256]{2,1,0:T(8,128)S(1)}, u32[]{:S(2)}, u32[]{:S(2)}) collective-permute-start(f32[5,8,256]{2,1,0:T(8,128)S(1)} %get-tuple-element.45), channel_id=1, source_target_pairs={{0,4},{1,5},{2,6},{3,7},{4,0},{5,1},{6,2},{7,3},{8,12},{9,13},{10,... | collective-permute-start | bytes 122888 | tf_op jit(solution)/shard_map/ppermute | solution.py:502
  41.3 4.4 %collective-permute-start.6 = (f32[6,8,256]{2,1,0:T(8,128)S(1)}, f32[6,8,256]{2,1,0:T(8,128)S(1)}, u32[]{:S(2)}, u32[]{:S(2)}) collective-permute-start(f32[6,8,256]{2,1,0:T(8,128)S(1)} %get-tuple-element.49), channel_id=1, source_target_pairs={{0,960},{64,0},{128,64},{192,128},{256,192},{320,256},{384,320},{4... | collective-permute-start | bytes 147464 | tf_op jit(solution)/shard_map/ppermute | solution.py:509
  45.7 1.9 %collective-permute-start.7 = (f32[6,8,256]{2,1,0:T(8,128)S(1)}, f32[6,8,256]{2,1,0:T(8,128)S(1)}, u32[]{:S(2)}, u32[]{:S(2)}) collective-permute-start(f32[6,8,256]{2,1,0:T(8,128)S(1)} %get-tuple-element.50), channel_id=1, source_target_pairs={{0,64},{64,128},{128,192},{192,256},{256,320},{320,384},{384,448},... | collective-permute-start | bytes 147464 | tf_op jit(solution)/shard_map/ppermute | solution.py:509
  47.6 0.0 collective-permute-done.rest_0_.rest_2_
  47.7 4.3 %collective-permute-start.3 = (f32[5,8,256]{2,1,0:T(8,128)S(1)}, f32[5,8,256]{2,1,0:T(8,128)S(1)}, u32[]{:S(2)}, u32[]{:S(2)}) collective-permute-start(f32[5,8,256]{2,1,0:T(8,128)S(1)} %get-tuple-element.46), channel_id=1, source_target_pairs={{0,8},{1,9},{2,10},{3,11},{4,12},{5,13},{6,14},{7,15},{8,0},{9,1},... | collective-permute-start | bytes 122888 | tf_op jit(solution)/shard_map/ppermute | solution.py:502
  52.0 0.0 collective-permute-done.1.rest_1_.rest_3_
  52.0 4.6 %collective-permute-start.4 = (f32[5,8,256]{2,1,0:T(8,128)S(1)}, f32[5,8,256]{2,1,0:T(8,128)S(1)}, u32[]{:S(2)}, u32[]{:S(2)}) collective-permute-start(f32[5,8,256]{2,1,0:T(8,128)S(1)} %get-tuple-element.47), channel_id=1, source_target_pairs={{0,1},{1,0},{2,3},{3,2},{4,5},{5,4},{6,7},{7,6},{8,9},{9,8},{10,11... | collective-permute-start | bytes 122888 | tf_op jit(solution)/shard_map/ppermute | solution.py:502
  56.6 0.0 collective-permute-done.2.rest_2_.rest_4_
  56.6 2.9 %collective-permute-start.5 = (f32[5,8,256]{2,1,0:T(8,128)S(1)}, f32[5,8,256]{2,1,0:T(8,128)S(1)}, u32[]{:S(2)}, u32[]{:S(2)}) collective-permute-start(f32[5,8,256]{2,1,0:T(8,128)S(1)} %get-tuple-element.48), channel_id=1, source_target_pairs={{0,2},{1,3},{2,0},{3,1},{4,6},{5,7},{6,4},{7,5},{8,10},{9,11},{10,... | collective-permute-start | bytes 122888 | tf_op jit(solution)/shard_map/ppermute | solution.py:502
  59.6 0.0 copy-done.2
  59.6 0.1 shard_map.60.clover
  59.6 0.0 collective-permute-done.3.rest_3_.rest_5_
  59.6 0.0 collective-permute-done.4.rest_4_.rest_6_
  59.7 2.9 %collective-permute-done.5.rest_5_.rest_7_ = f32[5,8,256]{2,1,0:T(8,128)S(1)} collective-permute-done((f32[5,8,256]{2,1,0:T(8,128)S(1)}, f32[5,8,256]{2,1,0:T(8,128)S(1)}, u32[]{:S(2)}, u32[]{:S(2)}) %collective-permute-start.5) | collective-permute-done | bytes 40992 | tf_op jit(solution)/shard_map/ppermute | solution.py:502
  62.5 0.0 collective-permute-done.6.rest_6_
  62.5 0.0 collective-permute-done.7.rest_7_
  62.5 1.0 shard_map.61
  63.5 8.4 %collective-permute-start.8 = (f32[6,8,256]{2,1,0:T(8,128)S(1)}, f32[6,8,256]{2,1,0:T(8,128)S(1)}, u32[]{:S(2)}, u32[]{:S(2)}) collective-permute-start(f32[6,8,256]{2,1,0:T(8,128)S(1)} %get-tuple-element.53), channel_id=1, source_target_pairs={{0,16},{1,17},{2,18},{3,19},{4,20},{5,21},{6,22},{7,23},{8,24},{9,... | collective-permute-start | bytes 147464 | tf_op jit(solution)/shard_map/ppermute | solution.py:502
  72.0 11.0 %collective-permute-start.9 = (f32[6,8,256]{2,1,0:T(8,128)S(1)}, f32[6,8,256]{2,1,0:T(8,128)S(1)}, u32[]{:S(2)}, u32[]{:S(2)}) collective-permute-start(f32[6,8,256]{2,1,0:T(8,128)S(1)} %get-tuple-element.54), channel_id=1, source_target_pairs={{0,32},{1,33},{2,34},{3,35},{4,36},{5,37},{6,38},{7,39},{8,40},{9,... | collective-permute-start | bytes 147464 | tf_op jit(solution)/shard_map/ppermute | solution.py:502
  83.0 6.9 %collective-permute-start.10 = (f32[6,8,256]{2,1,0:T(8,128)S(1)}, f32[6,8,256]{2,1,0:T(8,128)S(1)}, u32[]{:S(2)}, u32[]{:S(2)}) collective-permute-start(f32[6,8,256]{2,1,0:T(8,128)S(1)} %get-tuple-element.55), channel_id=1, source_target_pairs={{0,4},{1,5},{2,6},{3,7},{4,0},{5,1},{6,2},{7,3},{8,12},{9,13},{10,... | collective-permute-start | bytes 147464 | tf_op jit(solution)/shard_map/ppermute | solution.py:502
  90.0 1.9 %collective-permute-start.14 = (f32[12,8,256]{2,1,0:T(8,128)S(1)}, f32[12,8,256]{2,1,0:T(8,128)S(1)}, u32[]{:S(2)}, u32[]{:S(2)}) collective-permute-start(f32[12,8,256]{2,1,0:T(8,128)S(1)} %get-tuple-element.59), channel_id=1, source_target_pairs={{0,960},{64,0},{128,64},{192,128},{256,192},{320,256},{384,320},{4... | collective-permute-start | bytes 294920 | tf_op jit(solution)/shard_map/ppermute | solution.py:509
  91.9 2.4 %collective-permute-start.15 = (f32[12,8,256]{2,1,0:T(8,128)S(1)}, f32[12,8,256]{2,1,0:T(8,128)S(1)}, u32[]{:S(2)}, u32[]{:S(2)}) collective-permute-start(f32[12,8,256]{2,1,0:T(8,128)S(1)} %get-tuple-element.60), channel_id=1, source_target_pairs={{0,64},{64,128},{128,192},{192,256},{256,320},{320,384},{384,448},... | collective-permute-start | bytes 294920 | tf_op jit(solution)/shard_map/ppermute | solution.py:509
  94.3 0.0 collective-permute-done.8.rest_0_.rest_8_
  94.3 1.9 %collective-permute-start.11 = (f32[6,8,256]{2,1,0:T(8,128)S(1)}, f32[6,8,256]{2,1,0:T(8,128)S(1)}, u32[]{:S(2)}, u32[]{:S(2)}) collective-permute-start(f32[6,8,256]{2,1,0:T(8,128)S(1)} %get-tuple-element.56), channel_id=1, source_target_pairs={{0,8},{1,9},{2,10},{3,11},{4,12},{5,13},{6,14},{7,15},{8,0},{9,1},... | collective-permute-start | bytes 147464 | tf_op jit(solution)/shard_map/ppermute | solution.py:502
  96.2 4.9 %collective-permute-done.9.rest_1_.rest_9_ = f32[6,8,256]{2,1,0:T(8,128)S(1)} collective-permute-done((f32[6,8,256]{2,1,0:T(8,128)S(1)}, f32[6,8,256]{2,1,0:T(8,128)S(1)}, u32[]{:S(2)}, u32[]{:S(2)}) %collective-permute-start.9) | collective-permute-done | bytes 49184 | tf_op jit(solution)/shard_map/ppermute | solution.py:502
  101.2 2.8 %collective-permute-start.12 = (f32[6,8,256]{2,1,0:T(8,128)S(1)}, f32[6,8,256]{2,1,0:T(8,128)S(1)}, u32[]{:S(2)}, u32[]{:S(2)}) collective-permute-start(f32[6,8,256]{2,1,0:T(8,128)S(1)} %get-tuple-element.57), channel_id=1, source_target_pairs={{0,1},{1,0},{2,3},{3,2},{4,5},{5,4},{6,7},{7,6},{8,9},{9,8},{10,11... | collective-permute-start | bytes 147464 | tf_op jit(solution)/shard_map/ppermute | solution.py:502
  103.9 0.0 collective-permute-done.10.rest_2_.rest_10_
  103.9 1.9 %collective-permute-start.13 = (f32[6,8,256]{2,1,0:T(8,128)S(1)}, f32[6,8,256]{2,1,0:T(8,128)S(1)}, u32[]{:S(2)}, u32[]{:S(2)}) collective-permute-start(f32[6,8,256]{2,1,0:T(8,128)S(1)} %get-tuple-element.58), channel_id=1, source_target_pairs={{0,2},{1,3},{2,0},{3,1},{4,6},{5,7},{6,4},{7,5},{8,10},{9,11},{10,... | collective-permute-start | bytes 147464 | tf_op jit(solution)/shard_map/ppermute | solution.py:502
  105.9 0.0 collective-permute-done.11.rest_3_.rest_11_
  105.9 2.8 %collective-permute-done.12.rest_4_.rest_12_ = f32[6,8,256]{2,1,0:T(8,128)S(1)} collective-permute-done((f32[6,8,256]{2,1,0:T(8,128)S(1)}, f32[6,8,256]{2,1,0:T(8,128)S(1)}, u32[]{:S(2)}, u32[]{:S(2)}) %collective-permute-start.12) | collective-permute-done | bytes 49184 | tf_op jit(solution)/shard_map/ppermute | solution.py:502
  108.6 1.3 collective-permute-done.13.rest_5_.rest_13_
  109.9 0.0 collective-permute-done.14.rest_6_
  109.9 0.0 collective-permute-done.15.rest_7_
  109.9 1.5 shard_map.62
  111.5 1.9 %collective-permute-start.16 = (f32[12,8,256]{2,1,0:T(8,128)S(1)}, f32[12,8,256]{2,1,0:T(8,128)S(1)}, u32[]{:S(2)}, u32[]{:S(2)}) collective-permute-start(f32[12,8,256]{2,1,0:T(8,128)S(1)} %get-tuple-element.64), channel_id=1, source_target_pairs={{0,960},{64,0},{128,64},{192,128},{256,192},{320,256},{384,320},{4... | collective-permute-start | bytes 294920 | tf_op jit(solution)/shard_map/ppermute | solution.py:509
  113.4 2.4 %collective-permute-start.17 = (f32[12,8,256]{2,1,0:T(8,128)S(1)}, f32[12,8,256]{2,1,0:T(8,128)S(1)}, u32[]{:S(2)}, u32[]{:S(2)}) collective-permute-start(f32[12,8,256]{2,1,0:T(8,128)S(1)} %get-tuple-element.65), channel_id=1, source_target_pairs={{0,64},{64,128},{128,192},{192,256},{256,320},{320,384},{384,448},... | collective-permute-start | bytes 294920 | tf_op jit(solution)/shard_map/ppermute | solution.py:509
  115.8 0.0 collective-permute-done.16.rest_0_
  115.8 5.6 %collective-permute-done.17.rest_1_ = f32[12,8,256]{2,1,0:T(8,128)S(1)} collective-permute-done((f32[12,8,256]{2,1,0:T(8,128)S(1)}, f32[12,8,256]{2,1,0:T(8,128)S(1)}, u32[]{:S(2)}, u32[]{:S(2)}) %collective-permute-start.17) | collective-permute-done | bytes 98336 | tf_op jit(solution)/shard_map/ppermute | solution.py:509
  121.4 0.0 copy-done.1
  121.4 1.7 shard_map.63
  123.1 16.3 %all-to-all-start = ((f32[64,1,64]{2,1,0:T(1,128)}), f32[64,1,64]{2,1,0:T(1,128)S(1)}, u32[]{:S(2)}, u32[]{:S(2)}) async-start(f32[64,1,64]{2,1,0:T(1,128)} %bitcast.7), calls=%async_computation | async-start | bytes 65536 | tf_op jit(solution)/shard_map/all_to_all | solution.py:551
  139.5 12.1 %collective-permute-start.18 = (f32[2,8,256]{2,1,0:T(8,128)S(1)}, f32[2,8,256]{2,1,0:T(8,128)S(1)}, u32[]{:S(2)}, u32[]{:S(2)}) collective-permute-start(f32[2,8,256]{2,1,0:T(8,128)S(1)} %get-tuple-element.68), channel_id=1, source_target_pairs={{0,16},{1,17},{2,18},{3,19},{4,20},{5,21},{6,22},{7,23},{8,24},{9,... | collective-permute-start | bytes 49160 | tf_op jit(solution)/shard_map/ppermute | solution.py:502
  151.6 10.5 %collective-permute-start.19 = (f32[2,8,256]{2,1,0:T(8,128)S(1)}, f32[2,8,256]{2,1,0:T(8,128)S(1)}, u32[]{:S(2)}, u32[]{:S(2)}) collective-permute-start(f32[2,8,256]{2,1,0:T(8,128)S(1)} %get-tuple-element.69), channel_id=1, source_target_pairs={{0,32},{1,33},{2,34},{3,35},{4,36},{5,37},{6,38},{7,39},{8,40},{9,... | collective-permute-start | bytes 49160 | tf_op jit(solution)/shard_map/ppermute | solution.py:502
  162.1 4.2 %collective-permute-start.20 = (f32[2,8,256]{2,1,0:T(8,128)S(1)}, f32[2,8,256]{2,1,0:T(8,128)S(1)}, u32[]{:S(2)}, u32[]{:S(2)}) collective-permute-start(f32[2,8,256]{2,1,0:T(8,128)S(1)} %get-tuple-element.70), channel_id=1, source_target_pairs={{0,4},{1,5},{2,6},{3,7},{4,0},{5,1},{6,2},{7,3},{8,12},{9,13},{10,... | collective-permute-start | bytes 49160 | tf_op jit(solution)/shard_map/ppermute | solution.py:502
  166.3 2.5 %collective-permute-start.21 = (f32[2,8,256]{2,1,0:T(8,128)S(1)}, f32[2,8,256]{2,1,0:T(8,128)S(1)}, u32[]{:S(2)}, u32[]{:S(2)}) collective-permute-start(f32[2,8,256]{2,1,0:T(8,128)S(1)} %get-tuple-element.71), channel_id=1, source_target_pairs={{0,8},{1,9},{2,10},{3,11},{4,12},{5,13},{6,14},{7,15},{8,0},{9,1},... | collective-permute-start | bytes 49160 | tf_op jit(solution)/shard_map/ppermute | solution.py:502
  168.9 4.9 %collective-permute-start.22 = (f32[2,8,256]{2,1,0:T(8,128)S(1)}, f32[2,8,256]{2,1,0:T(8,128)S(1)}, u32[]{:S(2)}, u32[]{:S(2)}) collective-permute-start(f32[2,8,256]{2,1,0:T(8,128)S(1)} %get-tuple-element.72), channel_id=1, source_target_pairs={{0,1},{1,0},{2,3},{3,2},{4,5},{5,4},{6,7},{7,6},{8,9},{9,8},{10,11... | collective-permute-start | bytes 49160 | tf_op jit(solution)/shard_map/ppermute | solution.py:502
  173.7 0.0 collective-permute-done.18.rest_0_
  173.8 2.5 %collective-permute-start.23 = (f32[2,8,256]{2,1,0:T(8,128)S(1)}, f32[2,8,256]{2,1,0:T(8,128)S(1)}, u32[]{:S(2)}, u32[]{:S(2)}) collective-permute-start(f32[2,8,256]{2,1,0:T(8,128)S(1)} %get-tuple-element.73), channel_id=1, source_target_pairs={{0,2},{1,3},{2,0},{3,1},{4,6},{5,7},{6,4},{7,5},{8,10},{9,11},{10,... | collective-permute-start | bytes 49160 | tf_op jit(solution)/shard_map/ppermute | solution.py:502
  176.3 0.0 collective-permute-done.19.rest_1_
  176.3 0.0 collective-permute-done.20.rest_2_
  176.3 0.0 collective-permute-done.21.rest_3_
  176.3 0.0 collective-permute-done.22.rest_4_
  176.3 3.1 %collective-permute-done.23.rest_5_ = f32[2,8,256]{2,1,0:T(8,128)S(1)} collective-permute-done((f32[2,8,256]{2,1,0:T(8,128)S(1)}, f32[2,8,256]{2,1,0:T(8,128)S(1)}, u32[]{:S(2)}, u32[]{:S(2)}) %collective-permute-start.23) | collective-permute-done | bytes 16416 | tf_op jit(solution)/shard_map/ppermute | solution.py:502
  179.4 0.0 all-to-all-done
  179.4 1.0 shard_map.64
  (2 shorter events, 0.0 us)
Async XLA Ops:
  0.6 0.7 copy-start.4
  1.3 1.0 copy-start
  2.3 0.9 copy-start.3
  3.2 56.4 %copy-start.2 = (f32[1,2,2,6,6,216]{5,2,4,3,1,0:T(2,128)S(1)}, f32[1,2,2,6,6,216]{5,2,4,3,1,0:T(2,128)}, u32[]{:S(2)}) copy-start(f32[1,2,2,6,6,216]{5,2,4,3,1,0:T(2,128)} %param.7) | copy-start | bytes 373252
  4.6 43.1 %collective-permute-start = (f32[5,8,256]{2,1,0:T(8,128)S(1)}, f32[5,8,256]{2,1,0:T(8,128)S(1)}, u32[]{:S(2)}, u32[]{:S(2)}) collective-permute-start(f32[5,8,256]{2,1,0:T(8,128)S(1)} %get-tuple-element.43), channel_id=1, source_target_pairs={{0,16},{1,17},{2,18},{3,19},{4,20},{5,21},{6,22},{7,23},{8,24},{9,... | collective-permute-start | bytes 122888 | tf_op jit(solution)/shard_map/ppermute | solution.py:502
  20.3 31.6 %collective-permute-start.1 = (f32[5,8,256]{2,1,0:T(8,128)S(1)}, f32[5,8,256]{2,1,0:T(8,128)S(1)}, u32[]{:S(2)}, u32[]{:S(2)}) collective-permute-start(f32[5,8,256]{2,1,0:T(8,128)S(1)} %get-tuple-element.44), channel_id=1, source_target_pairs={{0,32},{1,33},{2,34},{3,35},{4,36},{5,37},{6,38},{7,39},{8,40},{9,... | collective-permute-start | bytes 122888 | tf_op jit(solution)/shard_map/ppermute | solution.py:502
  37.9 18.7 %collective-permute-start.2 = (f32[5,8,256]{2,1,0:T(8,128)S(1)}, f32[5,8,256]{2,1,0:T(8,128)S(1)}, u32[]{:S(2)}, u32[]{:S(2)}) collective-permute-start(f32[5,8,256]{2,1,0:T(8,128)S(1)} %get-tuple-element.45), channel_id=1, source_target_pairs={{0,4},{1,5},{2,6},{3,7},{4,0},{5,1},{6,2},{7,3},{8,12},{9,13},{10,... | collective-permute-start | bytes 122888 | tf_op jit(solution)/shard_map/ppermute | solution.py:502
  41.3 21.3 %collective-permute-start.6 = (f32[6,8,256]{2,1,0:T(8,128)S(1)}, f32[6,8,256]{2,1,0:T(8,128)S(1)}, u32[]{:S(2)}, u32[]{:S(2)}) collective-permute-start(f32[6,8,256]{2,1,0:T(8,128)S(1)} %get-tuple-element.49), channel_id=1, source_target_pairs={{0,960},{64,0},{128,64},{192,128},{256,192},{320,256},{384,320},{4... | collective-permute-start | bytes 147464 | tf_op jit(solution)/shard_map/ppermute | solution.py:509
  45.7 16.8 %collective-permute-start.7 = (f32[6,8,256]{2,1,0:T(8,128)S(1)}, f32[6,8,256]{2,1,0:T(8,128)S(1)}, u32[]{:S(2)}, u32[]{:S(2)}) collective-permute-start(f32[6,8,256]{2,1,0:T(8,128)S(1)} %get-tuple-element.50), channel_id=1, source_target_pairs={{0,64},{64,128},{128,192},{192,256},{256,320},{320,384},{384,448},... | collective-permute-start | bytes 147464 | tf_op jit(solution)/shard_map/ppermute | solution.py:509
  47.7 12.0 %collective-permute-start.3 = (f32[5,8,256]{2,1,0:T(8,128)S(1)}, f32[5,8,256]{2,1,0:T(8,128)S(1)}, u32[]{:S(2)}, u32[]{:S(2)}) collective-permute-start(f32[5,8,256]{2,1,0:T(8,128)S(1)} %get-tuple-element.46), channel_id=1, source_target_pairs={{0,8},{1,9},{2,10},{3,11},{4,12},{5,13},{6,14},{7,15},{8,0},{9,1},... | collective-permute-start | bytes 122888 | tf_op jit(solution)/shard_map/ppermute | solution.py:502
  52.0 7.7 %collective-permute-start.4 = (f32[5,8,256]{2,1,0:T(8,128)S(1)}, f32[5,8,256]{2,1,0:T(8,128)S(1)}, u32[]{:S(2)}, u32[]{:S(2)}) collective-permute-start(f32[5,8,256]{2,1,0:T(8,128)S(1)} %get-tuple-element.47), channel_id=1, source_target_pairs={{0,1},{1,0},{2,3},{3,2},{4,5},{5,4},{6,7},{7,6},{8,9},{9,8},{10,11... | collective-permute-start | bytes 122888 | tf_op jit(solution)/shard_map/ppermute | solution.py:502
  56.6 5.9 %collective-permute-start.5 = (f32[5,8,256]{2,1,0:T(8,128)S(1)}, f32[5,8,256]{2,1,0:T(8,128)S(1)}, u32[]{:S(2)}, u32[]{:S(2)}) collective-permute-start(f32[5,8,256]{2,1,0:T(8,128)S(1)} %get-tuple-element.48), channel_id=1, source_target_pairs={{0,2},{1,3},{2,0},{3,1},{4,6},{5,7},{6,4},{7,5},{8,10},{9,11},{10,... | collective-permute-start | bytes 122888 | tf_op jit(solution)/shard_map/ppermute | solution.py:502
  63.5 30.8 %collective-permute-start.8 = (f32[6,8,256]{2,1,0:T(8,128)S(1)}, f32[6,8,256]{2,1,0:T(8,128)S(1)}, u32[]{:S(2)}, u32[]{:S(2)}) collective-permute-start(f32[6,8,256]{2,1,0:T(8,128)S(1)} %get-tuple-element.53), channel_id=1, source_target_pairs={{0,16},{1,17},{2,18},{3,19},{4,20},{5,21},{6,22},{7,23},{8,24},{9,... | collective-permute-start | bytes 147464 | tf_op jit(solution)/shard_map/ppermute | solution.py:502
  72.0 29.2 %collective-permute-start.9 = (f32[6,8,256]{2,1,0:T(8,128)S(1)}, f32[6,8,256]{2,1,0:T(8,128)S(1)}, u32[]{:S(2)}, u32[]{:S(2)}) collective-permute-start(f32[6,8,256]{2,1,0:T(8,128)S(1)} %get-tuple-element.54), channel_id=1, source_target_pairs={{0,32},{1,33},{2,34},{3,35},{4,36},{5,37},{6,38},{7,39},{8,40},{9,... | collective-permute-start | bytes 147464 | tf_op jit(solution)/shard_map/ppermute | solution.py:502
  83.0 20.9 %collective-permute-start.10 = (f32[6,8,256]{2,1,0:T(8,128)S(1)}, f32[6,8,256]{2,1,0:T(8,128)S(1)}, u32[]{:S(2)}, u32[]{:S(2)}) collective-permute-start(f32[6,8,256]{2,1,0:T(8,128)S(1)} %get-tuple-element.55), channel_id=1, source_target_pairs={{0,4},{1,5},{2,6},{3,7},{4,0},{5,1},{6,2},{7,3},{8,12},{9,13},{10,... | collective-permute-start | bytes 147464 | tf_op jit(solution)/shard_map/ppermute | solution.py:502
  90.0 20.0 %collective-permute-start.14 = (f32[12,8,256]{2,1,0:T(8,128)S(1)}, f32[12,8,256]{2,1,0:T(8,128)S(1)}, u32[]{:S(2)}, u32[]{:S(2)}) collective-permute-start(f32[12,8,256]{2,1,0:T(8,128)S(1)} %get-tuple-element.59), channel_id=1, source_target_pairs={{0,960},{64,0},{128,64},{192,128},{256,192},{320,256},{384,320},{4... | collective-permute-start | bytes 294920 | tf_op jit(solution)/shard_map/ppermute | solution.py:509
  91.9 18.0 %collective-permute-start.15 = (f32[12,8,256]{2,1,0:T(8,128)S(1)}, f32[12,8,256]{2,1,0:T(8,128)S(1)}, u32[]{:S(2)}, u32[]{:S(2)}) collective-permute-start(f32[12,8,256]{2,1,0:T(8,128)S(1)} %get-tuple-element.60), channel_id=1, source_target_pairs={{0,64},{64,128},{128,192},{192,256},{256,320},{320,384},{384,448},... | collective-permute-start | bytes 294920 | tf_op jit(solution)/shard_map/ppermute | solution.py:509
  94.3 11.6 %collective-permute-start.11 = (f32[6,8,256]{2,1,0:T(8,128)S(1)}, f32[6,8,256]{2,1,0:T(8,128)S(1)}, u32[]{:S(2)}, u32[]{:S(2)}) collective-permute-start(f32[6,8,256]{2,1,0:T(8,128)S(1)} %get-tuple-element.56), channel_id=1, source_target_pairs={{0,8},{1,9},{2,10},{3,11},{4,12},{5,13},{6,14},{7,15},{8,0},{9,1},... | collective-permute-start | bytes 147464 | tf_op jit(solution)/shard_map/ppermute | solution.py:502
  101.2 7.5 %collective-permute-start.12 = (f32[6,8,256]{2,1,0:T(8,128)S(1)}, f32[6,8,256]{2,1,0:T(8,128)S(1)}, u32[]{:S(2)}, u32[]{:S(2)}) collective-permute-start(f32[6,8,256]{2,1,0:T(8,128)S(1)} %get-tuple-element.57), channel_id=1, source_target_pairs={{0,1},{1,0},{2,3},{3,2},{4,5},{5,4},{6,7},{7,6},{8,9},{9,8},{10,11... | collective-permute-start | bytes 147464 | tf_op jit(solution)/shard_map/ppermute | solution.py:502
  103.9 6.0 %collective-permute-start.13 = (f32[6,8,256]{2,1,0:T(8,128)S(1)}, f32[6,8,256]{2,1,0:T(8,128)S(1)}, u32[]{:S(2)}, u32[]{:S(2)}) collective-permute-start(f32[6,8,256]{2,1,0:T(8,128)S(1)} %get-tuple-element.58), channel_id=1, source_target_pairs={{0,2},{1,3},{2,0},{3,1},{4,6},{5,7},{6,4},{7,5},{8,10},{9,11},{10,... | collective-permute-start | bytes 147464 | tf_op jit(solution)/shard_map/ppermute | solution.py:502
  109.9 11.5 %copy-start.1 = (f32[2,3,1,64,216]{4,3,2,1,0:T(8,128)S(1)}, f32[2,3,1,64,216]{4,3,2,1,0:T(8,128)}, u32[]{:S(2)}) copy-start(f32[2,3,1,64,216]{4,3,2,1,0:T(8,128)} %param.5) | copy-start | bytes 995332
  111.5 4.3 %collective-permute-start.16 = (f32[12,8,256]{2,1,0:T(8,128)S(1)}, f32[12,8,256]{2,1,0:T(8,128)S(1)}, u32[]{:S(2)}, u32[]{:S(2)}) collective-permute-start(f32[12,8,256]{2,1,0:T(8,128)S(1)} %get-tuple-element.64), channel_id=1, source_target_pairs={{0,960},{64,0},{128,64},{192,128},{256,192},{320,256},{384,320},{4... | collective-permute-start | bytes 294920 | tf_op jit(solution)/shard_map/ppermute | solution.py:509
  113.4 8.0 %collective-permute-start.17 = (f32[12,8,256]{2,1,0:T(8,128)S(1)}, f32[12,8,256]{2,1,0:T(8,128)S(1)}, u32[]{:S(2)}, u32[]{:S(2)}) collective-permute-start(f32[12,8,256]{2,1,0:T(8,128)S(1)} %get-tuple-element.65), channel_id=1, source_target_pairs={{0,64},{64,128},{128,192},{192,256},{256,320},{320,384},{384,448},... | collective-permute-start | bytes 294920 | tf_op jit(solution)/shard_map/ppermute | solution.py:509
  123.1 56.3 %all-to-all-start = ((f32[64,1,64]{2,1,0:T(1,128)}), f32[64,1,64]{2,1,0:T(1,128)S(1)}, u32[]{:S(2)}, u32[]{:S(2)}) async-start(f32[64,1,64]{2,1,0:T(1,128)} %bitcast.7), calls=%async_computation | async-start | bytes 65536 | tf_op jit(solution)/shard_map/all_to_all | solution.py:551
  139.5 34.3 %collective-permute-start.18 = (f32[2,8,256]{2,1,0:T(8,128)S(1)}, f32[2,8,256]{2,1,0:T(8,128)S(1)}, u32[]{:S(2)}, u32[]{:S(2)}) collective-permute-start(f32[2,8,256]{2,1,0:T(8,128)S(1)} %get-tuple-element.68), channel_id=1, source_target_pairs={{0,16},{1,17},{2,18},{3,19},{4,20},{5,21},{6,22},{7,23},{8,24},{9,... | collective-permute-start | bytes 49160 | tf_op jit(solution)/shard_map/ppermute | solution.py:502
  151.6 24.7 %collective-permute-start.19 = (f32[2,8,256]{2,1,0:T(8,128)S(1)}, f32[2,8,256]{2,1,0:T(8,128)S(1)}, u32[]{:S(2)}, u32[]{:S(2)}) collective-permute-start(f32[2,8,256]{2,1,0:T(8,128)S(1)} %get-tuple-element.69), channel_id=1, source_target_pairs={{0,32},{1,33},{2,34},{3,35},{4,36},{5,37},{6,38},{7,39},{8,40},{9,... | collective-permute-start | bytes 49160 | tf_op jit(solution)/shard_map/ppermute | solution.py:502
  162.1 14.2 %collective-permute-start.20 = (f32[2,8,256]{2,1,0:T(8,128)S(1)}, f32[2,8,256]{2,1,0:T(8,128)S(1)}, u32[]{:S(2)}, u32[]{:S(2)}) collective-permute-start(f32[2,8,256]{2,1,0:T(8,128)S(1)} %get-tuple-element.70), channel_id=1, source_target_pairs={{0,4},{1,5},{2,6},{3,7},{4,0},{5,1},{6,2},{7,3},{8,12},{9,13},{10,... | collective-permute-start | bytes 49160 | tf_op jit(solution)/shard_map/ppermute | solution.py:502
  166.3 10.0 %collective-permute-start.21 = (f32[2,8,256]{2,1,0:T(8,128)S(1)}, f32[2,8,256]{2,1,0:T(8,128)S(1)}, u32[]{:S(2)}, u32[]{:S(2)}) collective-permute-start(f32[2,8,256]{2,1,0:T(8,128)S(1)} %get-tuple-element.71), channel_id=1, source_target_pairs={{0,8},{1,9},{2,10},{3,11},{4,12},{5,13},{6,14},{7,15},{8,0},{9,1},... | collective-permute-start | bytes 49160 | tf_op jit(solution)/shard_map/ppermute | solution.py:502
  168.9 7.4 %collective-permute-start.22 = (f32[2,8,256]{2,1,0:T(8,128)S(1)}, f32[2,8,256]{2,1,0:T(8,128)S(1)}, u32[]{:S(2)}, u32[]{:S(2)}) collective-permute-start(f32[2,8,256]{2,1,0:T(8,128)S(1)} %get-tuple-element.72), channel_id=1, source_target_pairs={{0,1},{1,0},{2,3},{3,2},{4,5},{5,4},{6,7},{7,6},{8,9},{9,8},{10,11... | collective-permute-start | bytes 49160 | tf_op jit(solution)/shard_map/ppermute | solution.py:502
  173.8 5.6 %collective-permute-start.23 = (f32[2,8,256]{2,1,0:T(8,128)S(1)}, f32[2,8,256]{2,1,0:T(8,128)S(1)}, u32[]{:S(2)}, u32[]{:S(2)}) collective-permute-start(f32[2,8,256]{2,1,0:T(8,128)S(1)} %get-tuple-element.73), channel_id=1, source_target_pairs={{0,2},{1,3},{2,0},{3,1},{4,6},{5,7},{6,4},{7,5},{8,10},{9,11},{10,... | collective-permute-start | bytes 49160 | tf_op jit(solution)/shard_map/ppermute | solution.py:502
